TPU v7x, 32 devices: a whole 2x2x4 slice. The times are simulated.
32 devices in a mesh: chan: 8 (over z, core), tm: 4 (over y, x).
Axes of the slice: x: 2, y: 2, z: 4, core: 2. Of those that a mesh axis runs over, the one named last changes fastest.
Arguments:
- spectra: float32 [32, 16, 2048], P('chan', 'tm'), as said below
- keep_mask: int32 [32, 16], P('chan', 'tm'), may hold values from 0 to 1, as said below
Outputs:
- stacked: float32 [32, 32, 201], P('chan', 'tm')
Inputs may be any that keep to these rules, and one draw needn't show every extreme that they name: `spectra`: real parts of the 1024 bins, then their imaginary parts, of each channel's and sub-window's spectrum. `keep_mask`: one or two channels are rejected in every sub-window; elsewhere the share of kept sub-windows rises along the time axis.
All inputs are finite; a program needn't handle non-finite values.
Results may differ from a plain program's by a relative error of at most 0.00066.
Values may be sent and summed in bfloat16 or wider, within the bound.
No kernel may reach another device: no remote copies, remote signals or barrier semaphores. Data moves between devices by JAX's collectives and lax.ppermute only.
A program may use at most 64 MiB of HBM per device.

v0:
```python
import jax
import jax.numpy as jnp
from jax import lax
from jax.sharding import PartitionSpec as P

F = 1024
MAXLAG = 100


def lag_table(nbins, maxlag):
    freq = jnp.arange(nbins, dtype=jnp.int32) + 1
    shift = jnp.arange(2 * maxlag + 1, dtype=jnp.int32) - maxlag
    turns = freq[:, None] * shift[None, :] % (2 * nbins)
    theta = turns.astype(jnp.float32) * (jnp.pi / nbins)
    return jnp.concatenate([jnp.cos(theta), -jnp.sin(theta)], axis=0) / nbins


def whiten(spectra):
    nbins = spectra.shape[-1] // 2
    real_part = spectra[..., :nbins]
    imag_part = spectra[..., nbins:]
    power = real_part * real_part + imag_part * imag_part
    level = jnp.mean(power, axis=-1, keepdims=True) + 1e-06
    factor = lax.rsqrt(power + 0.5 * level)
    return spectra * jnp.concatenate([factor, factor], axis=-1)


def correlate(table, near, near_mask, far, far_mask):
    nbins = near.shape[-1] // 2
    near_re = near[..., :nbins]
    near_im = near[..., nbins:]
    far_re = far[..., :nbins]
    far_im = far[..., nbins:]
    cross_re = jnp.einsum(
        "isf,jsf->ijf", near_re, far_re, preferred_element_type=jnp.float32
    ) + jnp.einsum("isf,jsf->ijf", near_im, far_im, preferred_element_type=jnp.float32)
    cross_im = jnp.einsum(
        "isf,jsf->ijf", near_im, far_re, preferred_element_type=jnp.float32
    ) - jnp.einsum("isf,jsf->ijf", near_re, far_im, preferred_element_type=jnp.float32)
    rows_near = near.shape[0]
    rows_far = far.shape[0]
    flat = jnp.concatenate([cross_re, cross_im], axis=-1).reshape(rows_near * rows_far, 2 * nbins)
    lagged = jnp.dot(flat, table, precision=lax.Precision.HIGHEST).reshape(
        rows_near, rows_far, table.shape[1]
    )
    pairs = jnp.dot(near_mask, far_mask.T, preferred_element_type=jnp.float32)
    return (lagged, pairs)


def local(spectra, keep_mask):
    table = lag_table(F, MAXLAG)
    maskf = keep_mask.astype(jnp.float32)
    white = (whiten(spectra) * maskf[:, :, None]).astype(jnp.bfloat16)
    mask_wire = keep_mask.astype(jnp.bfloat16)
    lagged, pairs = correlate(
        table,
        white,
        mask_wire,
        lax.all_gather(white, "chan", axis=0, tiled=True),
        lax.all_gather(mask_wire, "chan", axis=0, tiled=True),
    )
    summed = lagged
    counted = pairs
    summed, counted = (summed, counted)
    summed, counted = (
        lax.psum_scatter(summed, "tm", scatter_dimension=1, tiled=True),
        lax.psum_scatter(counted, "tm", scatter_dimension=1, tiled=True),
    )
    return summed / jnp.maximum(counted, 1.0)[:, :, None]


def solution(mesh):
    placed = (P("chan", "tm", None), P("chan", "tm"))
    return jax.shard_map(
        local, mesh=mesh, in_specs=placed, out_specs=P("chan", "tm", None), check_vma=False
    )
```

profile of v0, /device:TPU:0, one launch (start us, length us, event | category | flops | bytes accessed | tf_op | source)
XLA Modules:
  0.0 84.4 jit_solution(3740017134813775955)
XLA Ops:
  6.5 0.0 reduce-scatter.3.cloned.1.call-start
  6.5 0.8 convert_bitcast_fusion
  7.3 1.0 %fusion.19 = f32[4,4]{1,0:T(4,128)S(1)} fusion(f32[4,4,2048]{2,1,0:T(4,128)} %param.2), kind=kLoop, calls=%fused_computation.36 | loop fusion | flops 65520 | bytes 131136 | tf_op jit(solution)/shard_map/reduce_sum | solution.py:23
  8.3 1.0 %add_rsqrt_fusion = f32[4,4,1024]{2,1,0:T(4,128)S(1)} fusion(f32[4,4]{1,0:T(4,128)S(1)} %add_multiply_fusion, f32[4,4,2048]{2,1,0:T(4,128)} %param.2), kind=kLoop, calls=%fused_computation.24 | loop fusion | flops 65536 | bytes 196672 | tf_op jit(solution)/shard_map/rsqrt | solution.py:24
  9.3 1.0 %fusion.14 = bf16[4,4,2048]{2,1,0:T(4,128)(2,1)S(1)} fusion(f32[4,4,2048]{2,1,0:T(4,128)} %param.2, f32[4,4,1024]{2,1,0:T(4,128)S(1)} %add_rsqrt_fusion, f32[4,4]{1,0:T(4,128)S(1)} %get-tuple-element.12), kind=kLoop, calls=%fused_computation.23 | loop fusion | flops 131072 | bytes 262208 | tf_op jit(solution)/shard_map/convert_element_type | solution.py:53
  10.3 16.6 %all_gather.6 = bf16[32,4,2048]{2,1,0:T(4,128)(2,1)S(1)} all-gather(bf16[4,4,2048]{2,1,0:T(4,128)(2,1)S(1)} %fusion.14), channel_id=1, replica_groups=mesh['chan'=8,'tm'=4] {'chan'}, dimensions={0}, use_global_device_ids=true | all-gather | bytes 589824 | tf_op jit(solution)/shard_map/all_gather | solution.py:59
  26.9 0.2 fusion.20
  27.1 0.8 copy.38
  27.9 0.8 copy.27
  28.6 0.8 copy.39
  29.4 1.4 %copy.29 = bf16[4,4,1024]{1,0,2:T(4,128)(2,1)} copy(bf16[4,4,1024]{2,1,0:T(4,128)(2,1)S(1)} %get-tuple-element.8) | data formatting | bytes 65536 | tf_op jit(solution)/shard_map/slice | solution.py:31
  30.8 0.0 copy-start
  30.8 1.2 %fusion.22 = f32[1024,32,4]{1,2,0:T(4,128)S(1)} fusion(bf16[32,4,1024]{0,1,2:T(4,128)(2,1)S(1)} %copy.38, bf16[4,4,1024]{1,0,2:T(4,128)(2,1)S(1)} %copy.27), kind=kOutput, calls=%fused_computation.39 | convolution fusion | flops 1048576 | bytes 819200 | tf_op jit(solution)/shard_map/isf,jsf->ijf/dot_general | solution.py:34
  32.1 0.0 copy-done
  32.1 2.6 %fusion.23 = f32[1024,32,4]{1,2,0:T(4,128)} fusion(bf16[32,4,1024]{0,1,2:T(4,128)(2,1)S(1)} %copy.38, bf16[4,4,1024]{1,0,2:T(4,128)(2,1)S(1)} %copy-done), kind=kOutput, calls=%fused_computation.40 | convolution fusion | flops 1048576 | bytes 819200 | tf_op jit(solution)/shard_map/isf,jsf->ijf/dot_general | solution.py:37
  34.6 2.5 %add_bitcast_fusion = f32[4,32,1024]{1,0,2:T(4,128)} fusion(f32[1024,32,4]{1,2,0:T(4,128)S(1)} %fusion.22, bf16[32,4,1024]{0,1,2:T(4,128)(2,1)S(1)} %copy.39, bf16[4,4,1024]{1,0,2:T(4,128)(2,1)S(1)} %copy-done), kind=kOutput, calls=%fused_computation.1 | convolution fusion | flops 1179648 | bytes 1343488 | tf_op jit(solution)/shard_map/isf,jsf->ijf/dot_general | solution.py:36
  37.2 1.8 %copy.32 = f32[4,32,1024]{2,1,0:T(8,128)S(1)} copy(f32[4,32,1024]{1,0,2:T(4,128)} %add_bitcast_fusion) | data formatting | bytes 1048576 | tf_op jit(solution)/shard_map/add | solution.py:34
  39.0 4.2 %subtract_bitcast_fusion = f32[4,32,1024]{1,0,2:T(4,128)} fusion(f32[1024,32,4]{1,2,0:T(4,128)} %fusion.23, bf16[32,4,1024]{0,1,2:T(4,128)(2,1)S(1)} %copy.39, bf16[4,4,1024]{1,0,2:T(4,128)(2,1)S(1)} %copy.27), kind=kOutput, calls=%fused_computation | convolution fusion | flops 1179648 | bytes 1343488 | tf_op jit(solution)/shard_map/isf,jsf->ijf/dot_general | solution.py:39
  43.2 1.8 %copy.33 = f32[4,32,1024]{2,1,0:T(8,128)S(1)} copy(f32[4,32,1024]{1,0,2:T(4,128)} %subtract_bitcast_fusion) | data formatting | bytes 1048576 | tf_op jit(solution)/shard_map/sub | solution.py:37
  45.0 0.0 copy-start.1
  45.0 0.0 copy-start.2
  45.1 3.4 %fusion.12 = (f32[1024,201]{0,1:T(8,128)S(1)}, f32[1024,201]{0,1:T(8,128)S(1)}) fusion(s32[201]{0:T(256)S(1)} %iota_add_fusion.1, s32[1024]{0:T(1024)S(1)} %iota_add_fusion), kind=kLoop, calls=%fused_computation.20 | loop fusion | flops 3087360 | bytes 1651492 | tf_op jit(solution)/shard_map/cos | solution.py:15
  48.5 2.6 %fusion.1 = f32[4,32,201]{2,1,0:T(8,128)} fusion(f32[1024,201]{0,1:T(8,128)S(1)} %get-tuple-element.10, f32[1024,201]{0,1:T(8,128)S(1)} %get-tuple-element.9, f32[4,32,1024]{2,1,0:T(8,128)S(1)} %copy.33, f32[4,32,1024]{2,1,0:T(8,128)S(1)} %copy.32), kind=kOutput, calls=%fused_computation.4 | convolution fusion | flops 633376768 | bytes 2798080 | tf_op jit(solution)/shard_map/dot_general | solution.py:43
  51.0 0.0 reduce-scatter.3.cloned.1.call-update
  51.1 11.8 %all-gather = bf16[8,4,4]{2,1,0:T(4,128)(2,1)S(1)} all-gather(bf16[1,4,4]{2,1,0:T(4,128)(2,1)S(1)} %get-tuple-element.11), channel_id=1, replica_groups=mesh['chan'=8,'tm'=4] {'chan'}, dimensions={0}, use_global_device_ids=true | all-gather | bytes 288 | tf_op jit(solution)/shard_map/all_gather | solution.py:60
  62.8 0.0 copy-done.1
  62.8 0.1 fusion.15
  62.9 0.0 copy-done.2
  62.9 0.6 dynamic-slice
  64.2 10.0 %all-reduce = f32[4,32]{1,0:T(4,128)S(1)} all-reduce(f32[4,32]{1,0:T(4,128)S(1)} %fusion.15), channel_id=3, replica_groups=mesh['chan'=8,'tm'=4] {'tm'}, use_global_device_ids=true, to_apply=%region_2.3.clone | all-reduce | flops 128 | bytes 1024
  74.2 0.1 dynamic-slice_maximum_fusion
  74.2 1.9 %reduce-scatter.3.cloned.1.call-done = f32[4,8,201]{2,1,0:T(8,128)} async-done(((f32[4,32,201]{2,1,0:T(8,128)}), f32[4,8,201]{2,1,0:T(8,128)}) %reduce-scatter.3.cloned.1.call-update) | async-done | bytes 25744 | tf_op jit(solution)/shard_map/reduce_scatter | solution.py:66
  76.1 1.4 %broadcast_divide_fusion = f32[4,8,201]{2,1,0:T(8,128)} fusion(f32[4,8,201]{2,1,0:T(8,128)} %reduce-scatter.3.cloned.1.call-done, f32[4,8]{1,0:T(4,128)S(1)} %dynamic-slice_maximum_fusion), kind=kLoop, calls=%fused_computation.26 | loop fusion | flops 6432 | bytes 51584 | tf_op jit(solution)/shard_map/div | solution.py:69
  (4 shorter events, 0.0 us)
Async XLA Ops:
  6.5 69.6 %reduce-scatter.3.cloned.1.call-start = ((), (), s32[]{:S(2)}) async-start(), calls=%async_computation.1 | async-start | bytes 163840 | tf_op jit(solution)/shard_map/reduce_scatter | solution.py:66
  30.8 1.2 %copy-start = (bf16[4,4,1024]{1,0,2:T(4,128)(2,1)S(1)}, bf16[4,4,1024]{1,0,2:T(4,128)(2,1)}, u32[]{:S(2)}) copy-start(bf16[4,4,1024]{1,0,2:T(4,128)(2,1)} %copy.29) | copy-start | bytes 98308
  45.0 17.8 %copy-start.1 = (s32[4,4]{1,0:T(4,128)S(1)}, s32[4,4]{1,0:T(4,128)}, u32[]{:S(2)}) copy-start(s32[4,4]{1,0:T(4,128)} %param.3) | copy-start | bytes 196
  45.0 17.9 %copy-start.2 = (u32[32]{0:T(128)S(1)}, u32[32]{0:T(128)}, u32[]{:S(2)}) copy-start(u32[32]{0:T(128)} %constant.39) | copy-start | bytes 388
Sparse Core Ops, SparseCore 0:
  51.2 24.8 reduce-scatter.2
where the time goes:
time: 84.9 us; the launch traced here: 84.4 us
  blocking collectives  38.3 us (45%)
  between operations  14.2 us (17%)
  matrix products  13.2 us (16%)
  other arithmetic  8.64 us (10%)
  local copies, waits for them, and re-layouts  8.23 us (10%)
  waiting for transfers between devices  1.89 us (2%)
    all_gather x1, blocking collectives, local(): lax.all_gather(white, 'chan', axis=0, tiled=True)  16.6 us
    all_gather x1, blocking collectives, local(): lax.all_gather(mask_wire, 'chan', axis=0, tiled=True)  11.8 us
    unnamed x1, blocking collectives  9.97 us
    dot_general x1, matrix products, correlate(): jnp.einsum('isf,jsf->ijf', near_re, far_im, preferred_element_type=jnp.fl...  4.17 us
    cos x1, other arithmetic, lag_table(): return jnp.concatenate([jnp.cos(theta), -jnp.sin(theta)], axis=0) / nbins  3.4 us
    dot_general x1, matrix products, correlate(): jnp.einsum('isf,jsf->ijf', near_im, far_re, preferred_element_type=jnp.fl...  2.57 us
    dot_general x1, matrix products, correlate(): jnp.dot(flat, table, precision=lax.Precision.HIGHEST)  2.56 us
    dot_general x1, matrix products, correlate(): jnp.einsum('isf,jsf->ijf', near_im, far_im, preferred_element_type=jnp.fl...  2.53 us
  transfers between devices with their start and end apart: 1, of which 1 were waited for; matrix products, arithmetic and copies ran while one was open for 1% of the time, Pallas kernels for 0%

commit v1 on v0

v1 whole, which is shorter than its diff:
```python
import jax
import jax.numpy as jnp
import ml_dtypes
import numpy as np
from jax import lax
from jax.experimental import pallas as pl
from jax.experimental.pallas import tpu as pltpu
from jax.sharding import PartitionSpec as P

MAXLAG = 100
LANES = 128
CORES = 2
NUM_LAGS = 2 * MAXLAG + 1
PADDED_LAGS = 256


def lag_tables(nbins):
    freq = np.arange(nbins, dtype=np.int64) + 1
    shift = np.arange(NUM_LAGS, dtype=np.int64) - MAXLAG
    theta = (freq[:, None] * shift[None, :] % (2 * nbins)) * (np.pi / nbins)
    cosine = (np.cos(theta) / nbins).reshape(nbins // LANES, LANES, NUM_LAGS)
    sine = (-np.sin(theta) / nbins).reshape(nbins // LANES, LANES, NUM_LAGS)
    table = np.concatenate([cosine, sine], axis=1).astype(np.float32)
    table = np.pad(table, ((0, 0), (0, 0), (0, PADDED_LAGS - NUM_LAGS)))
    high = table.astype(ml_dtypes.bfloat16)
    low = (table - high.astype(np.float32)).astype(ml_dtypes.bfloat16)
    return high, low


def whiten_kernel(mask_ref, spectra_ref, out_ref):
    channels, windows, width = spectra_ref.shape
    nbins = width // 2
    blocks = width // LANES
    row = lax.broadcasted_iota(jnp.int32, (windows, 1), 0)
    pieces = []
    masks = []
    for ch in range(channels):
        keep = jnp.zeros((windows, 1), jnp.float32)
        for s in range(windows):
            keep = jnp.where(row == s, mask_ref[ch, s].astype(jnp.float32), keep)
        spec = spectra_ref[ch]
        re = spec[:, :nbins]
        im = spec[:, nbins:]
        power = re * re + im * im
        level = jnp.mean(power, axis=-1, keepdims=True) + 1e-06
        factor = lax.rsqrt(power + 0.5 * level)
        pieces.append((re * factor * keep, im * factor * keep))
        masks.append(jnp.broadcast_to(keep, (windows, LANES)))
    re = jnp.concatenate([p[0] for p in pieces], axis=0).astype(jnp.bfloat16)
    im = jnp.concatenate([p[1] for p in pieces], axis=0).astype(jnp.bfloat16)
    half = blocks // 2
    for fb in range(half):
        out_ref[fb] = re[:, fb * LANES : (fb + 1) * LANES]
        out_ref[half + fb] = im[:, fb * LANES : (fb + 1) * LANES]
    out_ref[blocks] = jnp.concatenate(masks, axis=0).astype(jnp.bfloat16)


def whiten(spectra, keep_mask):
    channels, windows, width = spectra.shape
    return pl.pallas_call(
        whiten_kernel,
        out_shape=jax.ShapeDtypeStruct((width // LANES + 1, channels * windows, LANES), jnp.bfloat16),
        in_specs=[pl.BlockSpec(memory_space=pltpu.SMEM), pl.BlockSpec(memory_space=pltpu.VMEM)],
        out_specs=pl.BlockSpec(memory_space=pltpu.VMEM),
        name="whiten",
    )(keep_mask, spectra)


def correlate_kernel(groups, channels, windows, *refs):
    place_ref = refs[0]
    near_refs = refs[1 : 1 + groups]
    far_refs = refs[1 + groups : 3 + groups]
    high_ref, low_ref, out_ref, pattern_ref, lag_ref, pair_ref = refs[3 + groups :]
    blocks = near_refs[0].shape[0] - 1
    half = blocks // 2
    duos = channels // 2
    rows = 2 * windows
    upper = lax.broadcasted_iota(jnp.int32, (rows, LANES), 0) < windows

    for k in range(groups):
        for fb in range(blocks + 1):
            wide = near_refs[k][fb].astype(jnp.float32)
            for duo in range(duos):
                tile = wide[duo * rows : (duo + 1) * rows]
                turned = pltpu.roll(tile, windows, 0)
                pattern_ref[k, fb, 2 * duo] = jnp.where(upper, tile, turned)
                pattern_ref[k, fb, 2 * duo + 1] = jnp.where(upper, turned, tile)

    swap = place_ref[0]
    total = jnp.zeros((channels * 2 * duos * rows, PADDED_LAGS), jnp.float32)
    for fb in range(half):
        lines = {}
        for side in range(2):
            acc = {}
            for b in range(groups):
                k = lax.bitwise_xor(swap, b)
                far_re = far_refs[side][b, fb].astype(jnp.float32)
                far_im = far_refs[side][b, half + fb].astype(jnp.float32)
                for i in range(channels):
                    near_re = pattern_ref[k, fb, i]
                    near_im = pattern_ref[k, half + fb, i]
                    for duo in range(duos):
                        fr = far_re[duo * rows : (duo + 1) * rows]
                        fi = far_im[duo * rows : (duo + 1) * rows]
                        re = near_re * fr + near_im * fi
                        im = near_im * fr - near_re * fi
                        if b:
                            re = acc[i, duo][0] + re
                            im = acc[i, duo][1] + im
                        acc[i, duo] = (re, im)
            for (i, duo), (re, im) in acc.items():
                lines[i, side, duo] = jnp.concatenate([re, im], axis=1)
        cross = jnp.concatenate([lines[key] for key in sorted(lines)], axis=0)
        top = cross.astype(jnp.bfloat16)
        rest = (cross - top.astype(jnp.float32)).astype(jnp.bfloat16)
        both = jnp.dot(jnp.concatenate([top, rest], axis=0), high_ref[fb], preferred_element_type=jnp.float32)
        size = cross.shape[0]
        total = total + (both[:size] + both[size:]) + jnp.dot(top, low_ref[fb], preferred_element_type=jnp.float32)
    for side in range(PADDED_LAGS // LANES):
        lag_ref[side] = total[:, side * LANES : (side + 1) * LANES]

    counts = {}
    for side in range(2):
        for b in range(groups):
            k = lax.bitwise_xor(swap, b)
            far = far_refs[side][b, blocks].astype(jnp.float32)
            for i in range(channels):
                near = pattern_ref[k, blocks, i]
                for duo in range(duos):
                    count = near * far[duo * rows : (duo + 1) * rows]
                    counts[i, side, duo] = counts[i, side, duo] + count if b else count
    pair_ref[...] = jnp.concatenate([counts[key] for key in sorted(counts)], axis=0)

    lines = channels * 2 * channels
    pairs = sum(pair_ref[pl.ds(s, lines, stride=windows), :] for s in range(windows))
    pairs = jnp.maximum(pairs, 1.0)
    parts = []
    for side in range(PADDED_LAGS // LANES):
        lag = sum(lag_ref[side, pl.ds(s, lines, stride=windows), :] for s in range(windows))
        parts.append(lag / pairs)
    result = jnp.concatenate(parts, axis=1)
    core = place_ref[1]
    for i in range(channels):
        block = result[i * 2 * channels : (i + 1) * 2 * channels]
        block = jnp.where(core == 0, block, pltpu.roll(block, channels, 0))
        out_ref[i] = block[:, :NUM_LAGS]


def correlate(place, near, far, channels, windows, tables):
    groups = len(near)
    blocks = near[0].shape[0]
    lines = channels * 2 * channels * windows
    vmem = pl.BlockSpec(memory_space=pltpu.VMEM)
    kernel = lambda *refs: correlate_kernel(groups, channels, windows, *refs)
    return pl.pallas_call(
        kernel,
        out_shape=jax.ShapeDtypeStruct((channels, 2 * channels, NUM_LAGS), jnp.float32),
        in_specs=[pl.BlockSpec(memory_space=pltpu.SMEM)] + [vmem] * (groups + 4),
        out_specs=vmem,
        scratch_shapes=[
            pltpu.VMEM((groups, blocks, channels, 2 * windows, LANES), jnp.float32),
            pltpu.VMEM((PADDED_LAGS // LANES, lines, LANES), jnp.float32),
            pltpu.VMEM((lines, LANES), jnp.float32),
        ],
        name="correlate",
    )(place, *near, *far, *tables)


def solution(mesh):
    groups = mesh.shape["tm"]
    assert mesh.shape["chan"] == CORES * groups and groups & (groups - 1) == 0

    def route(move):
        pairs = []
        for line in range(groups):
            for core in range(CORES):
                for t in range(groups):
                    to_line, to_core, to_t = move(line, core, t)
                    source = (line * CORES + core) * groups + t
                    pairs.append((source, (to_line * CORES + to_core) * groups + to_t))
        return pairs

    def send(value, move):
        return lax.ppermute(value, ("chan", "tm"), route(move))

    def local(spectra, keep_mask):
        channels, windows, width = spectra.shape
        own = whiten(spectra, keep_mask)
        far = [send(own, lambda line, core, t, b=b: (t ^ b, core, line)) for b in range(groups)]
        near = [own] + [send(own, lambda line, core, t, k=k: (line, core, t ^ k)) for k in range(1, groups)]
        *near, far = lax.optimization_barrier((*near, jnp.stack(far)))
        other = send(far, lambda line, core, t: (line, 1 - core, t))
        chan = lax.axis_index("chan")
        place = jnp.stack([(chan // CORES) ^ lax.axis_index("tm"), chan % CORES]).astype(jnp.int32)
        tables = [jnp.asarray(table) for table in lag_tables(width // 2)]
        return correlate(place, near, (far, other), channels, windows, tables)

    placed = (P("chan", "tm", None), P("chan", "tm"))
    return jax.shard_map(local, mesh=mesh, in_specs=placed, out_specs=P("chan", "tm", None), check_vma=False)
```

time: 84.9 us -> 26.1 us (0.31)
  blocking collectives: 38.3 us -> 0 us
  starting transfers between devices: 0.01 us -> 14.3 us
  between operations: 14.2 us -> 0.07 us
  matrix products: 13.2 us -> 0 us
  other arithmetic: 8.64 us -> 0.69 us
  local copies, waits for them, and re-layouts: 8.23 us -> 0.73 us
  Pallas kernels: 0 us -> 5.13 us
  waiting for transfers between devices: 1.89 us -> 4.77 us
    all_gather x2 -> x0, blocking collectives: 28.3 us -> none  [the longest x1 16.6 us: local(): lax.all_gather(white, 'chan', axis=0, tiled=True)]
    ppermute x0 -> x8, starting transfers between devices: none -> 14.3 us  [send(): return lax.ppermute(value, ('chan', 'tm'), route(move))]
    dot_general x6 -> x0, matrix products: 13.2 us -> none  [the longest x1 4.17 us: correlate(): jnp.einsum('isf,jsf->ijf', near_re, far_im, preferred_element_type=jnp.fl...]
    unnamed x1 -> x0, blocking collectives: 9.97 us -> none
    pallas_call x0 -> x2, Pallas kernels: none -> 5.13 us  [the longest x1 3.47 us: correlate(): pl.pallas_call(kernel, out_shape=jax.ShapeDtypeStruct((channels, 2 * chan...]
    ppermute x0 -> x8, waiting for transfers between devices: none -> 4.77 us  [send(): return lax.ppermute(value, ('chan', 'tm'), route(move))]
    cos x1 -> x0, other arithmetic: 3.4 us -> none  [lag_table(): return jnp.concatenate([jnp.cos(theta), -jnp.sin(theta)], axis=0) / nbins]
    slice x4 -> x0, local copies, waits for them, and re-layouts: 2.39 us -> none  [the longest x1 1.43 us: correlate(): near_im = near[..., nbins:]]
  transfers between devices with their start and end apart: 1 -> 8, of which waited for: 1 -> 4; matrix products, arithmetic and copies ran while one was open for 1% -> 3% of each run, Pallas kernels for 0% -> 0%
where the time goes in v1:
time: 26.1 us; the launch traced here: 25.7 us
  starting transfers between devices  14.3 us (55%)
  Pallas kernels  5.13 us (20%)
  waiting for transfers between devices  4.77 us (18%)
  local copies, waits for them, and re-layouts  0.73 us (3%)
  other arithmetic  0.69 us (3%)
    ppermute x8, starting transfers between devices, send(): return lax.ppermute(value, ('chan', 'tm'), route(move))  14.3 us
    ppermute x8, waiting for transfers between devices, send(): return lax.ppermute(value, ('chan', 'tm'), route(move))  4.77 us
    pallas_call x1, Pallas kernels, correlate(): pl.pallas_call(kernel, out_shape=jax.ShapeDtypeStruct((channels, 2 * chan...  3.47 us
    pallas_call x1, Pallas kernels, whiten(): pl.pallas_call(whiten_kernel, out_shape=jax.ShapeDtypeStruct((width // LA...  1.65 us
    unnamed x10, local copies, waits for them, and re-layouts  0.73 us
    another operation x1, other arithmetic, local(): jnp.stack([chan // CORES ^ lax.axis_index('tm'), chan % CORES])  0.65 us
  transfers between devices with their start and end apart: 8, of which 4 were waited for; matrix products, arithmetic and copies ran while one was open for 3% of the time, Pallas kernels for 0%

profile of v1, /device:TPU:0, one launch (start us, length us, event | category | flops | bytes accessed | tf_op | source)
XLA Modules:
  0.0 25.7 jit_solution(17637795979454917019)
XLA Ops:
  0.0 1.7 %whiten.1.refs_1_ = bf16[17,16,128]{2,1,0:T(8,128)(2,1)} custom-call(s32[4,4]{1,0:T(4,128)} %mask_ref.1, f32[4,4,2048]{2,1,0:T(4,128)} %spectra_ref.1), custom_call_target="tpu_custom_call" | custom-call | tf_op jit(solution)/shard_map/whiten/pallas_call | solution.py:60
  1.7 5.0 %collective-permute-start.6 = (bf16[17,16,128]{2,1,0:T(8,128)(2,1)}, bf16[17,16,128]{2,1,0:T(8,128)(2,1)S(1)}, u32[]{:S(2)}, u32[]{:S(2)}) collective-permute-start(bf16[17,16,128]{2,1,0:T(8,128)(2,1)} %whiten.1.refs_1_), channel_id=1, source_target_pairs={{0,24},{1,16},{2,8},{3,0},{4,28},{5,20},{6,12},{7,4},{8,25},{9,17}... | collective-permute-start | bytes 208904 | tf_op jit(solution)/shard_map/ppermute | solution.py:184
  6.7 1.5 %collective-permute-start.5 = (bf16[17,16,128]{2,1,0:T(8,128)(2,1)}, bf16[17,16,128]{2,1,0:T(8,128)(2,1)S(1)}, u32[]{:S(2)}, u32[]{:S(2)}) collective-permute-start(bf16[17,16,128]{2,1,0:T(8,128)(2,1)} %whiten.1.refs_1_), channel_id=1, source_target_pairs={{0,16},{1,24},{2,0},{3,8},{4,20},{5,28},{6,4},{7,12},{8,17},{9,25}... | collective-permute-start | bytes 208904 | tf_op jit(solution)/shard_map/ppermute | solution.py:184
  8.2 0.5 %collective-permute-start.4 = (bf16[17,16,128]{2,1,0:T(8,128)(2,1)}, bf16[17,16,128]{2,1,0:T(8,128)(2,1)S(1)}, u32[]{:S(2)}, u32[]{:S(2)}) collective-permute-start(bf16[17,16,128]{2,1,0:T(8,128)(2,1)} %whiten.1.refs_1_), channel_id=1, source_target_pairs={{0,8},{1,0},{2,24},{3,16},{4,12},{5,4},{6,28},{7,20},{8,9},{9,1},{... | collective-permute-start | bytes 208904 | tf_op jit(solution)/shard_map/ppermute | solution.py:184
  8.7 1.5 %collective-permute-start.3 = (bf16[17,16,128]{2,1,0:T(8,128)(2,1)}, bf16[17,16,128]{2,1,0:T(8,128)(2,1)S(1)}, u32[]{:S(2)}, u32[]{:S(2)}) collective-permute-start(bf16[17,16,128]{2,1,0:T(8,128)(2,1)} %whiten.1.refs_1_), channel_id=1, source_target_pairs={{0,0},{1,8},{2,16},{3,24},{4,4},{5,12},{6,20},{7,28},{8,1},{9,9},{... | collective-permute-start | bytes 208904 | tf_op jit(solution)/shard_map/ppermute | solution.py:184
  10.2 5.1 %collective-permute-start.2 = (bf16[17,16,128]{2,1,0:T(8,128)(2,1)}, bf16[17,16,128]{2,1,0:T(8,128)(2,1)S(1)}, u32[]{:S(2)}, u32[]{:S(2)}) collective-permute-start(bf16[17,16,128]{2,1,0:T(8,128)(2,1)} %whiten.1.refs_1_), channel_id=1, source_target_pairs={{0,3},{1,2},{2,1},{3,0},{4,7},{5,6},{6,5},{7,4},{8,11},{9,10},{10,... | collective-permute-start | bytes 208904 | tf_op jit(solution)/shard_map/ppermute | solution.py:184
  15.3 0.0 collective-permute-done.6
  15.3 0.0 collective-permute-start.1
  15.3 0.0 collective-permute-done.5
  15.4 0.6 %collective-permute-start = (bf16[17,16,128]{2,1,0:T(8,128)(2,1)}, bf16[17,16,128]{2,1,0:T(8,128)(2,1)S(1)}, u32[]{:S(2)}, u32[]{:S(2)}) collective-permute-start(bf16[17,16,128]{2,1,0:T(8,128)(2,1)} %whiten.1.refs_1_), channel_id=1, source_target_pairs={{0,1},{1,0},{2,3},{3,2},{4,5},{5,4},{6,7},{7,6},{8,9},{9,8},{10,11... | collective-permute-start | bytes 208904 | tf_op jit(solution)/shard_map/ppermute | solution.py:184
  16.0 0.0 collective-permute-done.4
  16.0 0.0 collective-permute-done.3
  16.0 0.0 copy-start
  16.1 2.9 %collective-permute-done.2.refs_4_ = bf16[17,16,128]{2,1,0:T(8,128)(2,1)S(1)} collective-permute-done((bf16[17,16,128]{2,1,0:T(8,128)(2,1)}, bf16[17,16,128]{2,1,0:T(8,128)(2,1)S(1)}, u32[]{:S(2)}, u32[]{:S(2)}) %collective-permute-start.2) | collective-permute-done | bytes 69664 | tf_op jit(solution)/shard_map/ppermute | solution.py:184
  19.0 0.0 copy-start.2
  19.0 0.9 %collective-permute-done.1.refs_3_ = bf16[17,16,128]{2,1,0:T(8,128)(2,1)S(1)} collective-permute-done((bf16[17,16,128]{2,1,0:T(8,128)(2,1)}, bf16[17,16,128]{2,1,0:T(8,128)(2,1)S(1)}, u32[]{:S(2)}, u32[]{:S(2)}) %collective-permute-start.1) | collective-permute-done | bytes 69664 | tf_op jit(solution)/shard_map/ppermute | solution.py:184
  19.9 0.0 copy-start.3
  19.9 0.1 collective-permute-done.refs_2_
  19.9 0.0 copy-start.4
  19.9 0.0 collective-permute-start.7
  20.0 0.7 %pad_add_fusion.refs_0_ = s32[2]{0:T(128)} fusion(s32[1]{0:T(128)} %bitcast.1, s32[1]{0:T(128)} %bitcast), kind=kLoop, calls=%fused_computation.1 | loop fusion | flops 2 | bytes 16 | tf_op jit(solution)/shard_map/stack | solution.py:194
  20.6 0.9 %collective-permute-done.7.refs_6_ = bf16[4,17,16,128]{3,2,1,0:T(8,128)(2,1)S(1)} collective-permute-done((bf16[4,17,16,128]{3,2,1,0:T(8,128)(2,1)S(1)}, bf16[4,17,16,128]{3,2,1,0:T(8,128)(2,1)S(1)}, u32[]{:S(2)}, u32[]{:S(2)}) %collective-permute-start.7) | collective-permute-done | bytes 278560 | tf_op jit(solution)/shard_map/ppermute | solution.py:184
  21.5 0.0 copy-done
  21.5 0.0 copy-done.2
  21.5 0.0 copy-done.3
  21.5 0.0 copy-done.4
  21.5 0.0 copy-start.1
  21.5 0.7 %copy-done.1 = bf16[4,17,16,128]{3,2,1,0:T(8,128)(2,1)} copy-done((bf16[4,17,16,128]{3,2,1,0:T(8,128)(2,1)}, bf16[4,17,16,128]{3,2,1,0:T(8,128)(2,1)S(1)}, u32[]{:S(2)}) %copy-start.1) | copy-done | bytes 278552
  22.2 3.5 %correlate.1 = f32[4,8,201]{2,1,0:T(8,128)} custom-call(s32[2]{0:T(128)} %pad_add_fusion.refs_0_, bf16[17,16,128]{2,1,0:T(8,128)(2,1)} %whiten.1.refs_1_, bf16[17,16,128]{2,1,0:T(8,128)(2,1)} %copy-done.4, bf16[17,16,128]{2,1,0:T(8,128)(2,1)} %copy-done.3, bf16[17,16,128]{2,1,0:T(8,128)(2,1)} %copy-done.2, bf16[4,17,16,128]{3,2,1,0:T(8,128)(2,1)} %copy-done, ...), custom_call_target="tpu_custom_call" | custom-call | tf_op jit(solution)/shard_map/correlate/pallas_call | solution.py:155
  (1 shorter events, 0.0 us)
Async XLA Ops:
  1.7 13.7 %collective-permute-start.6 = (bf16[17,16,128]{2,1,0:T(8,128)(2,1)}, bf16[17,16,128]{2,1,0:T(8,128)(2,1)S(1)}, u32[]{:S(2)}, u32[]{:S(2)}) collective-permute-start(bf16[17,16,128]{2,1,0:T(8,128)(2,1)} %whiten.1.refs_1_), channel_id=1, source_target_pairs={{0,24},{1,16},{2,8},{3,0},{4,28},{5,20},{6,12},{7,4},{8,25},{9,17}... | collective-permute-start | bytes 208904 | tf_op jit(solution)/shard_map/ppermute | solution.py:184
  6.7 8.6 %collective-permute-start.5 = (bf16[17,16,128]{2,1,0:T(8,128)(2,1)}, bf16[17,16,128]{2,1,0:T(8,128)(2,1)S(1)}, u32[]{:S(2)}, u32[]{:S(2)}) collective-permute-start(bf16[17,16,128]{2,1,0:T(8,128)(2,1)} %whiten.1.refs_1_), channel_id=1, source_target_pairs={{0,16},{1,24},{2,0},{3,8},{4,20},{5,28},{6,4},{7,12},{8,17},{9,25}... | collective-permute-start | bytes 208904 | tf_op jit(solution)/shard_map/ppermute | solution.py:184
  8.2 7.8 %collective-permute-start.4 = (bf16[17,16,128]{2,1,0:T(8,128)(2,1)}, bf16[17,16,128]{2,1,0:T(8,128)(2,1)S(1)}, u32[]{:S(2)}, u32[]{:S(2)}) collective-permute-start(bf16[17,16,128]{2,1,0:T(8,128)(2,1)} %whiten.1.refs_1_), channel_id=1, source_target_pairs={{0,8},{1,0},{2,24},{3,16},{4,12},{5,4},{6,28},{7,20},{8,9},{9,1},{... | collective-permute-start | bytes 208904 | tf_op jit(solution)/shard_map/ppermute | solution.py:184
  8.7 7.3 %collective-permute-start.3 = (bf16[17,16,128]{2,1,0:T(8,128)(2,1)}, bf16[17,16,128]{2,1,0:T(8,128)(2,1)S(1)}, u32[]{:S(2)}, u32[]{:S(2)}) collective-permute-start(bf16[17,16,128]{2,1,0:T(8,128)(2,1)} %whiten.1.refs_1_), channel_id=1, source_target_pairs={{0,0},{1,8},{2,16},{3,24},{4,4},{5,12},{6,20},{7,28},{8,1},{9,9},{... | collective-permute-start | bytes 208904 | tf_op jit(solution)/shard_map/ppermute | solution.py:184
  10.2 8.8 %collective-permute-start.2 = (bf16[17,16,128]{2,1,0:T(8,128)(2,1)}, bf16[17,16,128]{2,1,0:T(8,128)(2,1)S(1)}, u32[]{:S(2)}, u32[]{:S(2)}) collective-permute-start(bf16[17,16,128]{2,1,0:T(8,128)(2,1)} %whiten.1.refs_1_), channel_id=1, source_target_pairs={{0,3},{1,2},{2,1},{3,0},{4,7},{5,6},{6,5},{7,4},{8,11},{9,10},{10,... | collective-permute-start | bytes 208904 | tf_op jit(solution)/shard_map/ppermute | solution.py:184
  15.3 4.5 %collective-permute-start.1 = (bf16[17,16,128]{2,1,0:T(8,128)(2,1)}, bf16[17,16,128]{2,1,0:T(8,128)(2,1)S(1)}, u32[]{:S(2)}, u32[]{:S(2)}) collective-permute-start(bf16[17,16,128]{2,1,0:T(8,128)(2,1)} %whiten.1.refs_1_), channel_id=1, source_target_pairs={{0,2},{1,3},{2,0},{3,1},{4,6},{5,7},{6,4},{7,5},{8,10},{9,11},{10,... | collective-permute-start | bytes 208904 | tf_op jit(solution)/shard_map/ppermute | solution.py:184
  15.4 4.6 %collective-permute-start = (bf16[17,16,128]{2,1,0:T(8,128)(2,1)}, bf16[17,16,128]{2,1,0:T(8,128)(2,1)S(1)}, u32[]{:S(2)}, u32[]{:S(2)}) collective-permute-start(bf16[17,16,128]{2,1,0:T(8,128)(2,1)} %whiten.1.refs_1_), channel_id=1, source_target_pairs={{0,1},{1,0},{2,3},{3,2},{4,5},{5,4},{6,7},{7,6},{8,9},{9,8},{10,11... | collective-permute-start | bytes 208904 | tf_op jit(solution)/shard_map/ppermute | solution.py:184
  16.0 5.5 %copy-start = (bf16[4,17,16,128]{3,2,1,0:T(8,128)(2,1)}, bf16[4,17,16,128]{3,2,1,0:T(8,128)(2,1)S(1)}, u32[]{:S(2)}) copy-start(bf16[4,17,16,128]{3,2,1,0:T(8,128)(2,1)S(1)} %pad_maximum_fusion.refs_5_) | copy-start | bytes 835588
  19.0 2.5 %copy-start.2 = (bf16[17,16,128]{2,1,0:T(8,128)(2,1)}, bf16[17,16,128]{2,1,0:T(8,128)(2,1)S(1)}, u32[]{:S(2)}) copy-start(bf16[17,16,128]{2,1,0:T(8,128)(2,1)S(1)} %collective-permute-done.2.refs_4_) | copy-start | bytes 208900
  19.9 1.6 %copy-start.3 = (bf16[17,16,128]{2,1,0:T(8,128)(2,1)}, bf16[17,16,128]{2,1,0:T(8,128)(2,1)S(1)}, u32[]{:S(2)}) copy-start(bf16[17,16,128]{2,1,0:T(8,128)(2,1)S(1)} %collective-permute-done.1.refs_3_) | copy-start | bytes 208900
  19.9 1.6 %copy-start.4 = (bf16[17,16,128]{2,1,0:T(8,128)(2,1)}, bf16[17,16,128]{2,1,0:T(8,128)(2,1)S(1)}, u32[]{:S(2)}) copy-start(bf16[17,16,128]{2,1,0:T(8,128)(2,1)S(1)} %collective-permute-done.refs_2_) | copy-start | bytes 208900
  19.9 1.6 %collective-permute-start.7 = (bf16[4,17,16,128]{3,2,1,0:T(8,128)(2,1)S(1)}, bf16[4,17,16,128]{3,2,1,0:T(8,128)(2,1)S(1)}, u32[]{:S(2)}, u32[]{:S(2)}) collective-permute-start(bf16[4,17,16,128]{3,2,1,0:T(8,128)(2,1)S(1)} %pad_maximum_fusion.refs_5_), channel_id=1, source_target_pairs={{0,4},{1,5},{2,6},{3,7},{4,0},{5,1},{6,2},{7,3},{8,12},{9,13},{10,... | collective-permute-start | bytes 835592 | tf_op jit(solution)/shard_map/ppermute | solution.py:184
  21.5 0.7 %copy-start.1 = (bf16[4,17,16,128]{3,2,1,0:T(8,128)(2,1)}, bf16[4,17,16,128]{3,2,1,0:T(8,128)(2,1)S(1)}, u32[]{:S(2)}) copy-start(bf16[4,17,16,128]{3,2,1,0:T(8,128)(2,1)S(1)} %collective-permute-done.7.refs_6_) | copy-start | bytes 835588

commit v2 on v1

v2 whole, which is shorter than its diff:
```python
import jax
import jax.numpy as jnp
import ml_dtypes
import numpy as np
from jax import lax
from jax.experimental import pallas as pl
from jax.experimental.pallas import tpu as pltpu
from jax.sharding import PartitionSpec as P

MAXLAG = 100
LANES = 128
CORES = 2
NUM_LAGS = 2 * MAXLAG + 1
PADDED_LAGS = 256
BEHIND = 0
VMEM_LIMIT = 32 << 20


def lag_table(nbins):
    freq = np.arange(nbins, dtype=np.int64) + 1
    shift = np.arange(NUM_LAGS, dtype=np.int64) - MAXLAG
    theta = (freq[:, None] * shift[None, :] % (2 * nbins)) * (np.pi / nbins)
    cosine = (np.cos(theta) / nbins).reshape(nbins // LANES, LANES, NUM_LAGS)
    sine = (-np.sin(theta) / nbins).reshape(nbins // LANES, LANES, NUM_LAGS)
    table = np.concatenate([cosine, sine], axis=1).astype(np.float32)
    table = np.pad(table, ((0, 0), (0, 0), (0, PADDED_LAGS - NUM_LAGS)))
    high = table.astype(ml_dtypes.bfloat16)
    low = (table - high.astype(np.float32)).astype(ml_dtypes.bfloat16)
    return np.stack([high, low], axis=1)


def whiten_kernel(mask_ref, spectra_ref, out_ref):
    channels, windows, width = spectra_ref.shape
    nbins = width // 2
    blocks = width // LANES
    row = lax.broadcasted_iota(jnp.int32, (windows, 1), 0)
    pieces = []
    masks = []
    for ch in range(channels):
        keep = jnp.zeros((windows, 1), jnp.float32)
        for s in range(windows):
            keep = jnp.where(row == s, mask_ref[ch, s].astype(jnp.float32), keep)
        spec = spectra_ref[ch]
        re = spec[:, :nbins]
        im = spec[:, nbins:]
        power = re * re + im * im
        level = jnp.mean(power, axis=-1, keepdims=True) + 1e-06
        factor = lax.rsqrt(power + 0.5 * level)
        pieces.append((re * factor * keep, im * factor * keep))
        masks.append(jnp.broadcast_to(keep, (windows, LANES)))
    re = jnp.concatenate([p[0] for p in pieces], axis=0).astype(jnp.bfloat16)
    im = jnp.concatenate([p[1] for p in pieces], axis=0).astype(jnp.bfloat16)
    half = blocks // 2
    for fb in range(half):
        out_ref[fb] = re[:, fb * LANES : (fb + 1) * LANES]
        out_ref[half + fb] = im[:, fb * LANES : (fb + 1) * LANES]
    out_ref[blocks] = jnp.concatenate(masks, axis=0).astype(jnp.bfloat16)


def whiten(spectra, keep_mask):
    channels, windows, width = spectra.shape
    return pl.pallas_call(
        whiten_kernel,
        out_shape=pltpu.VMEM((width // LANES + 1, channels * windows, LANES), jnp.bfloat16),
        in_specs=[pl.BlockSpec(memory_space=pltpu.SMEM), pl.BlockSpec(memory_space=pltpu.VMEM)],
        out_specs=pl.BlockSpec(memory_space=pltpu.VMEM),
        compiler_params=pltpu.CompilerParams(vmem_limit_bytes=VMEM_LIMIT),
        name="whiten",
    )(keep_mask, spectra)


def hold_kernel(table_ref, held_ref, arrived):
    fetches = [pltpu.make_async_copy(table_ref.at[n], held_ref.at[n], arrived.at[n]) for n in range(table_ref.shape[0])]
    for fetch in fetches:
        fetch.start()
    for fetch in fetches:
        fetch.wait()


def hold(table):
    return pl.pallas_call(
        hold_kernel,
        out_shape=pltpu.VMEM(table.shape, table.dtype),
        in_specs=[pl.BlockSpec(memory_space=pl.ANY)],
        out_specs=pl.BlockSpec(memory_space=pltpu.VMEM),
        scratch_shapes=[pltpu.SemaphoreType.DMA((table.shape[0],))],
        compiler_params=pltpu.CompilerParams(vmem_limit_bytes=VMEM_LIMIT),
        name="hold",
    )(table)


def exchange_plan(groups):
    far = [(("far", b), ("far", groups - 1 - b)) for b in range(groups // 2)]
    near = [(("near", k), ("near", groups - 1 - k)) for k in range(1, groups // 2)]
    return far + near + [(("near", groups - 1), ("near", groups - 1))]


def passes(blocks):
    return blocks[0] != blocks[1] or blocks[0][0] == "far"


def correlate_kernel(groups, channels, windows, *refs):
    plan = exchange_plan(groups)
    refs = list(refs)
    take = lambda count: [refs.pop(0) for _ in range(count)]
    (own_ref,), direct_refs = take(1), take(len(plan))
    passed_refs = {n: refs.pop(0) for n in range(len(plan)) if passes(plan[n])}
    held_ref, out_ref, pattern_ref, lag_ref, pair_ref = refs
    blocks = own_ref.shape[0] - 1
    half = blocks // 2
    duos = channels // 2
    rows = 2 * windows
    chan = lax.axis_index("chan")
    core = lax.rem(chan, CORES)
    swap = lax.bitwise_xor(lax.div(chan, CORES), lax.axis_index("tm"))

    wide = lambda ref: lambda fb: ref[fb].astype(jnp.float32)
    either = lambda ref, other: lambda fb: jnp.where(core == 0, ref[fb], other[fb]).astype(jnp.float32)
    near_loads = [(0, wide(own_ref))]
    upper = lax.broadcasted_iota(jnp.int32, (rows, LANES), 0) < windows
    far_loads = [[], []]
    for n, (block, other) in enumerate(plan):
        direct, passed = direct_refs[n], passed_refs.get(n)
        if block == other:
            if block[0] == "near":
                near_loads.append((block[1], wide(direct)))
            else:
                slot = lax.bitwise_xor(swap, block[1])
                far_loads[0].append((slot, wide(direct)))
                far_loads[1].append((slot, wide(passed)))
            continue
        turn = core * (block[1] ^ other[1])
        mine, theirs = lax.bitwise_xor(turn, block[1]), lax.bitwise_xor(turn, other[1])
        if block[0] == "near":
            near_loads += [(mine, wide(direct.at[0])), (theirs, wide(passed))]
        elif other[0] == "far":
            for side in range(2):
                far_loads[side].append((lax.bitwise_xor(swap, mine), wide(direct.at[side])))
                far_loads[side].append((lax.bitwise_xor(swap, theirs), wide(passed.at[1 - side])))
        else:
            near_loads.append((other[1], either(passed.at[1], direct.at[0])))
            for side in range(2):
                slot = lax.bitwise_xor(swap, block[1])
                far_loads[side].append((slot, either(direct.at[side], passed.at[1 - side])))

    for slot, load in near_loads:
        for fb in range(blocks + 1):
            block = load(fb)
            for duo in range(duos):
                tile = block[duo * rows : (duo + 1) * rows]
                turned = pltpu.roll(tile, windows, 0)
                pattern_ref[slot, fb, 2 * duo] = jnp.where(upper, tile, turned)
                pattern_ref[slot, fb, 2 * duo + 1] = jnp.where(upper, turned, tile)

    crosses = []

    def transform(fb):
        cross = crosses[fb]
        size = cross.shape[0]
        top = cross.astype(jnp.bfloat16)
        rest = (cross - top.astype(jnp.float32)).astype(jnp.bfloat16)
        both = jnp.dot(jnp.concatenate([top, rest], axis=0), held_ref[fb, 0], preferred_element_type=jnp.float32)
        return both[:size] + both[size:] + jnp.dot(top, held_ref[fb, 1], preferred_element_type=jnp.float32)

    total = jnp.zeros((channels * 2 * duos * rows, PADDED_LAGS), jnp.float32)
    for fb in range(half):
        lines = {}
        for side in range(2):
            acc = {}
            for n, (k, load) in enumerate(far_loads[side]):
                far_re = load(fb)
                far_im = load(half + fb)
                for i in range(channels):
                    near_re = pattern_ref[k, fb, i]
                    near_im = pattern_ref[k, half + fb, i]
                    for duo in range(duos):
                        fr = far_re[duo * rows : (duo + 1) * rows]
                        fi = far_im[duo * rows : (duo + 1) * rows]
                        re = near_re * fr + near_im * fi
                        im = near_im * fr - near_re * fi
                        if n:
                            re = acc[i, duo][0] + re
                            im = acc[i, duo][1] + im
                        acc[i, duo] = (re, im)
            for (i, duo), (re, im) in acc.items():
                lines[i, side, duo] = jnp.concatenate([re, im], axis=1)
        crosses.append(jnp.concatenate([lines[key] for key in sorted(lines)], axis=0))
        if fb >= BEHIND:
            total = total + transform(fb - BEHIND)
    for fb in range(half - BEHIND, half):
        total = total + transform(fb)
    for side in range(PADDED_LAGS // LANES):
        lag_ref[side] = total[:, side * LANES : (side + 1) * LANES]

    counts = {}
    for side in range(2):
        for n, (k, load) in enumerate(far_loads[side]):
            far = load(blocks)
            for i in range(channels):
                near = pattern_ref[k, blocks, i]
                for duo in range(duos):
                    count = near * far[duo * rows : (duo + 1) * rows]
                    counts[i, side, duo] = counts[i, side, duo] + count if n else count
    pair_ref[...] = jnp.concatenate([counts[key] for key in sorted(counts)], axis=0)

    lines = channels * 2 * channels
    pairs = sum(pair_ref[pl.ds(s, lines, stride=windows), :] for s in range(windows))
    pairs = jnp.maximum(pairs, 1.0)
    parts = []
    for side in range(PADDED_LAGS // LANES):
        lag = sum(lag_ref[side, pl.ds(s, lines, stride=windows), :] for s in range(windows))
        parts.append(lag / pairs)
    result = jnp.concatenate(parts, axis=1)
    for i in range(channels):
        block = result[i * 2 * channels : (i + 1) * 2 * channels]
        block = jnp.where(core == 0, block, pltpu.roll(block, channels, 0))
        out_ref[i] = block[:, :NUM_LAGS]


def correlate(groups, spectra, channels, windows, table):
    blocks = spectra[0].shape[0]
    lines = channels * 2 * channels * windows
    vmem = pl.BlockSpec(memory_space=pltpu.VMEM)
    kernel = lambda *refs: correlate_kernel(groups, channels, windows, *refs)
    held = [pltpu.with_memory_space_constraint(value, pltpu.VMEM) for value in (*spectra, table)]
    return pl.pallas_call(
        kernel,
        out_shape=jax.ShapeDtypeStruct((channels, 2 * channels, NUM_LAGS), jnp.float32),
        in_specs=[vmem] * len(held),
        out_specs=vmem,
        scratch_shapes=[
            pltpu.VMEM((groups, blocks, channels, 2 * windows, LANES), jnp.float32),
            pltpu.VMEM((PADDED_LAGS // LANES, lines, LANES), jnp.float32),
            pltpu.VMEM((lines, LANES), jnp.float32),
        ],
        compiler_params=pltpu.CompilerParams(vmem_limit_bytes=VMEM_LIMIT),
        name="correlate",
    )(*held)


def solution(mesh):
    groups = mesh.shape["tm"]
    assert mesh.shape["chan"] == CORES * groups and groups & (groups - 1) == 0

    def route(move):
        pairs = []
        for line in range(groups):
            for core in range(CORES):
                for t in range(groups):
                    to_line, to_core, to_t = move(line, core, t)
                    source = (line * CORES + core) * groups + t
                    pairs.append((source, (to_line * CORES + to_core) * groups + to_t))
        return pairs

    def send(value, move):
        return lax.ppermute(value, ("chan", "tm"), route(move))

    def local(spectra, keep_mask):
        channels, windows, width = spectra.shape
        swap = lambda value: send(value, lambda line, core, t: (line, 1 - core, t))
        swap = lambda value: send(value, lambda line, core, t: (line, 1 - core, t))
        moves = {
            "far": lambda line, core, t, b: (t ^ b, core, line),
            "near": lambda line, core, t, k: (line, core, t ^ k),
        }

        def fetch(value, *blocks):
            def move(line, core, t):
                kind, number = blocks[core]
                return moves[kind](line, core, t, number)

            return send(value, move)

        own = whiten(spectra, keep_mask)
        chip = jnp.stack([own, swap(own)])
        plan = exchange_plan(groups)
        direct = [fetch(own if blocks[0] == blocks[1] else chip, *blocks) for blocks in plan]
        passed = []
        for blocks, value in zip(plan, direct):
            if passes(blocks):
                half = blocks[0] != blocks[1] and blocks[0][0] == "near"
                passed.append(swap(value[1] if half else value))
        table = hold(jnp.asarray(lag_table(width // 2)))
        received = (own, *direct, *passed)
        return correlate(groups, received, channels, windows, table)

    placed = (P("chan", "tm", None), P("chan", "tm"))
    return jax.shard_map(local, mesh=mesh, in_specs=placed, out_specs=P("chan", "tm", None), check_vma=False)
```

time: 26.1 us -> 22 us (0.84)
  the two profiles are of different devices: /device:TPU:0 before, /device:TPU:5 now
where the time goes in v2:
time: 22 us; the launch traced here: 21.9 us
  starting transfers between devices  14.4 us (65%)
  local copies, waits for them, and re-layouts  3.18 us (14%)
  Pallas kernels  2.58 us (12%)
  waiting for transfers between devices  1.64 us (7%)
    ppermute x8, starting transfers between devices, send(): return lax.ppermute(value, ('chan', 'tm'), route(move))  14.4 us
    unnamed x6, local copies, waits for them, and re-layouts  3.17 us
    pallas_call x1, Pallas kernels, correlate(): pl.pallas_call(kernel, out_shape=jax.ShapeDtypeStruct((channels, 2 * chan...  1.66 us
    ppermute x8, waiting for transfers between devices, send(): return lax.ppermute(value, ('chan', 'tm'), route(move))  1.64 us
    pallas_call x1, Pallas kernels, whiten(): pl.pallas_call(whiten_kernel, out_shape=pltpu.VMEM((width // LANES + 1, c...  0.69 us
  transfers between devices with their start and end apart: 8, of which 2 were waited for; matrix products, arithmetic and copies ran while one was open for 0% of the time, Pallas kernels for 1%

profile of v2, /device:TPU:5, one launch (start us, length us, event | category | flops | bytes accessed | tf_op | source)
XLA Modules:
  0.0 21.9 jit_solution(314218002835714235)
XLA Ops:
  0.0 0.0 copy-start.1
  0.0 0.9 %copy-done.1 = f32[4,4,2048]{2,1,0:T(4,128)S(1)} copy-done((f32[4,4,2048]{2,1,0:T(4,128)S(1)}, f32[4,4,2048]{2,1,0:T(4,128)}, u32[]{:S(2)}) %copy-start.1) | copy-done | bytes 131096
  0.9 0.0 copy-start.2
  0.9 0.7 %copy-done.2 = s32[4,4]{1,0:T(4,128)S(1)} copy-done((s32[4,4]{1,0:T(4,128)S(1)}, s32[4,4]{1,0:T(4,128)}, u32[]{:S(2)}) %copy-start.2) | copy-done | bytes 88
  1.6 0.7 %whiten.1.refs_0_ = bf16[17,16,128]{2,1,0:T(8,128)(2,1)S(1)} custom-call(s32[4,4]{1,0:T(4,128)S(1)} %copy-done.2, f32[4,4,2048]{2,1,0:T(4,128)S(1)} %copy-done.1), custom_call_target="tpu_custom_call" | custom-call | tf_op jit(solution)/shard_map/whiten/pallas_call | solution.py:62
  2.3 0.7 %collective-permute-start = (bf16[17,16,128]{2,1,0:T(8,128)(2,1)S(1)}, bf16[17,16,128]{2,1,0:T(8,128)(2,1)S(1)}, u32[]{:S(2)}, u32[]{:S(2)}) collective-permute-start(bf16[17,16,128]{2,1,0:T(8,128)(2,1)S(1)} %whiten.1.refs_0_), channel_id=1, source_target_pairs={{0,4},{1,5},{2,6},{3,7},{4,0},{5,1},{6,2},{7,3},{8,12},{9,13},{10,... | collective-permute-start | bytes 208904 | tf_op jit(solution)/shard_map/ppermute | solution.py:256
  3.0 0.9 %collective-permute-done = bf16[17,16,128]{2,1,0:T(8,128)(2,1)S(1)} collective-permute-done((bf16[17,16,128]{2,1,0:T(8,128)(2,1)S(1)}, bf16[17,16,128]{2,1,0:T(8,128)(2,1)S(1)}, u32[]{:S(2)}, u32[]{:S(2)}) %collective-permute-start) | collective-permute-done | bytes 69664 | tf_op jit(solution)/shard_map/ppermute | solution.py:256
  3.9 0.1 collective-permute-start.2
  4.0 5.3 %collective-permute-start.1 = (bf16[2,17,16,128]{3,2,1,0:T(8,128)(2,1)S(1)}, bf16[2,17,16,128]{3,2,1,0:T(8,128)(2,1)S(1)}, u32[]{:S(2)}, u32[]{:S(2)}) collective-permute-start(bf16[2,17,16,128]{3,2,1,0:T(8,128)(2,1)S(1)} %pad_maximum_fusion), channel_id=1, source_target_pairs={{0,0},{1,8},{2,16},{3,24},{4,28},{5,20},{6,12},{7,4},{8,1},{9,9},{... | collective-permute-start | bytes 417800 | tf_op jit(solution)/shard_map/ppermute | solution.py:256
  9.4 2.2 %collective-permute-start.3 = (bf16[2,17,16,128]{3,2,1,0:T(8,128)(2,1)S(1)}, bf16[2,17,16,128]{3,2,1,0:T(8,128)(2,1)S(1)}, u32[]{:S(2)}, u32[]{:S(2)}) collective-permute-start(bf16[2,17,16,128]{3,2,1,0:T(8,128)(2,1)S(1)} %pad_maximum_fusion), channel_id=1, source_target_pairs={{0,1},{1,0},{2,3},{3,2},{4,6},{5,7},{6,4},{7,5},{8,9},{9,8},{10,11... | collective-permute-start | bytes 417800 | tf_op jit(solution)/shard_map/ppermute | solution.py:256
  11.6 0.0 collective-permute-start.4
  11.6 0.0 collective-permute-done.2.refs_2_
  11.6 2.2 %collective-permute-start.6 = (bf16[2,17,16,128]{3,2,1,0:T(8,128)(2,1)S(1)}, bf16[2,17,16,128]{3,2,1,0:T(8,128)(2,1)S(1)}, u32[]{:S(2)}, u32[]{:S(2)}) collective-permute-start(bf16[2,17,16,128]{3,2,1,0:T(8,128)(2,1)S(1)} %collective-permute-done.2.refs_2_), channel_id=1, source_target_pairs={{0,4},{1,5},{2,6},{3,7},{4,0},{5,1},{6,2},{7,3},{8,12},{9,13},{10,... | collective-permute-start | bytes 417800 | tf_op jit(solution)/shard_map/ppermute | solution.py:256
  13.8 0.7 %collective-permute-done.1.refs_1_ = bf16[2,17,16,128]{3,2,1,0:T(8,128)(2,1)S(1)} collective-permute-done((bf16[2,17,16,128]{3,2,1,0:T(8,128)(2,1)S(1)}, bf16[2,17,16,128]{3,2,1,0:T(8,128)(2,1)S(1)}, u32[]{:S(2)}, u32[]{:S(2)}) %collective-permute-start.1) | collective-permute-done | bytes 139296 | tf_op jit(solution)/shard_map/ppermute | solution.py:256
  14.5 3.7 %collective-permute-start.5 = (bf16[2,17,16,128]{3,2,1,0:T(8,128)(2,1)S(1)}, bf16[2,17,16,128]{3,2,1,0:T(8,128)(2,1)S(1)}, u32[]{:S(2)}, u32[]{:S(2)}) collective-permute-start(bf16[2,17,16,128]{3,2,1,0:T(8,128)(2,1)S(1)} %collective-permute-done.1.refs_1_), channel_id=1, source_target_pairs={{0,4},{1,5},{2,6},{3,7},{4,0},{5,1},{6,2},{7,3},{8,12},{9,13},{10,... | collective-permute-start | bytes 417800 | tf_op jit(solution)/shard_map/ppermute | solution.py:256
  18.2 0.0 collective-permute-done.3.refs_3_
  18.2 0.1 collective-permute-start.7
  18.3 0.0 copy-start
  18.3 1.6 %copy-done = bf16[8,2,256,256]{3,2,1,0:T(8,128)(2,1)S(1)} copy-done((bf16[8,2,256,256]{3,2,1,0:T(8,128)(2,1)S(1)}, bf16[8,2,256,256]{3,2,1,0:T(8,128)(2,1)}, u32[]{:S(2)}) %copy-start) | copy-done | bytes 2097176
  19.9 0.2 %hold.1.refs_8_ = bf16[8,2,256,256]{3,2,1,0:T(8,128)(2,1)S(1)} custom-call(bf16[8,2,256,256]{3,2,1,0:T(8,128)(2,1)S(1)} %copy-done), custom_call_target="tpu_custom_call" | custom-call | tf_op jit(solution)/shard_map/hold/pallas_call | solution.py:81
  20.2 0.0 collective-permute-done.4.refs_4_
  20.2 0.0 collective-permute-done.7.refs_7_
  20.2 0.0 collective-permute-done.6.refs_6_
  20.2 0.0 collective-permute-done.5.refs_5_
  20.2 1.7 %correlate.1 = f32[4,8,201]{2,1,0:T(8,128)} custom-call(bf16[17,16,128]{2,1,0:T(8,128)(2,1)S(1)} %whiten.1.refs_0_, bf16[2,17,16,128]{3,2,1,0:T(8,128)(2,1)S(1)} %collective-permute-done.1.refs_1_, bf16[2,17,16,128]{3,2,1,0:T(8,128)(2,1)S(1)} %collective-permute-done.2.refs_2_, bf16[2,17,16,128]{3,2,1,0:T(8,128)(2,1)S(1)} %collective-permute-done.3.refs_3_, ...), custom_call_target="tpu_custom_call" | custom-call | tf_op jit(solution)/shard_map/correlate/pallas_call | solution.py:226
  (2 shorter events, 0.0 us)
Async XLA Ops:
  0.0 0.9 %copy-start.1 = (f32[4,4,2048]{2,1,0:T(4,128)S(1)}, f32[4,4,2048]{2,1,0:T(4,128)}, u32[]{:S(2)}) copy-start(f32[4,4,2048]{2,1,0:T(4,128)} %spectra_ref.1) | copy-start | bytes 393220
  0.9 0.7 %copy-start.2 = (s32[4,4]{1,0:T(4,128)S(1)}, s32[4,4]{1,0:T(4,128)}, u32[]{:S(2)}) copy-start(s32[4,4]{1,0:T(4,128)} %mask_ref.1) | copy-start | bytes 196
  2.3 1.6 %collective-permute-start = (bf16[17,16,128]{2,1,0:T(8,128)(2,1)S(1)}, bf16[17,16,128]{2,1,0:T(8,128)(2,1)S(1)}, u32[]{:S(2)}, u32[]{:S(2)}) collective-permute-start(bf16[17,16,128]{2,1,0:T(8,128)(2,1)S(1)} %whiten.1.refs_0_), channel_id=1, source_target_pairs={{0,4},{1,5},{2,6},{3,7},{4,0},{5,1},{6,2},{7,3},{8,12},{9,13},{10,... | collective-permute-start | bytes 208904 | tf_op jit(solution)/shard_map/ppermute | solution.py:256
  3.9 7.6 %collective-permute-start.2 = (bf16[2,17,16,128]{3,2,1,0:T(8,128)(2,1)S(1)}, bf16[2,17,16,128]{3,2,1,0:T(8,128)(2,1)S(1)}, u32[]{:S(2)}, u32[]{:S(2)}) collective-permute-start(bf16[2,17,16,128]{3,2,1,0:T(8,128)(2,1)S(1)} %pad_maximum_fusion), channel_id=1, source_target_pairs={{0,8},{1,0},{2,24},{3,16},{4,20},{5,28},{6,4},{7,12},{8,9},{9,1},{... | collective-permute-start | bytes 417800 | tf_op jit(solution)/shard_map/ppermute | solution.py:256
  4.0 10.5 %collective-permute-start.1 = (bf16[2,17,16,128]{3,2,1,0:T(8,128)(2,1)S(1)}, bf16[2,17,16,128]{3,2,1,0:T(8,128)(2,1)S(1)}, u32[]{:S(2)}, u32[]{:S(2)}) collective-permute-start(bf16[2,17,16,128]{3,2,1,0:T(8,128)(2,1)S(1)} %pad_maximum_fusion), channel_id=1, source_target_pairs={{0,0},{1,8},{2,16},{3,24},{4,28},{5,20},{6,12},{7,4},{8,1},{9,9},{... | collective-permute-start | bytes 417800 | tf_op jit(solution)/shard_map/ppermute | solution.py:256
  9.4 8.9 %collective-permute-start.3 = (bf16[2,17,16,128]{3,2,1,0:T(8,128)(2,1)S(1)}, bf16[2,17,16,128]{3,2,1,0:T(8,128)(2,1)S(1)}, u32[]{:S(2)}, u32[]{:S(2)}) collective-permute-start(bf16[2,17,16,128]{3,2,1,0:T(8,128)(2,1)S(1)} %pad_maximum_fusion), channel_id=1, source_target_pairs={{0,1},{1,0},{2,3},{3,2},{4,6},{5,7},{6,4},{7,5},{8,9},{9,8},{10,11... | collective-permute-start | bytes 417800 | tf_op jit(solution)/shard_map/ppermute | solution.py:256
  11.6 8.6 %collective-permute-start.4 = (bf16[17,16,128]{2,1,0:T(8,128)(2,1)S(1)}, bf16[17,16,128]{2,1,0:T(8,128)(2,1)S(1)}, u32[]{:S(2)}, u32[]{:S(2)}) collective-permute-start(bf16[17,16,128]{2,1,0:T(8,128)(2,1)S(1)} %whiten.1.refs_0_), channel_id=1, source_target_pairs={{0,3},{1,2},{2,1},{3,0},{4,7},{5,6},{6,5},{7,4},{8,11},{9,10},{10,... | collective-permute-start | bytes 208904 | tf_op jit(solution)/shard_map/ppermute | solution.py:256
  11.6 8.6 %collective-permute-start.6 = (bf16[2,17,16,128]{3,2,1,0:T(8,128)(2,1)S(1)}, bf16[2,17,16,128]{3,2,1,0:T(8,128)(2,1)S(1)}, u32[]{:S(2)}, u32[]{:S(2)}) collective-permute-start(bf16[2,17,16,128]{3,2,1,0:T(8,128)(2,1)S(1)} %collective-permute-done.2.refs_2_), channel_id=1, source_target_pairs={{0,4},{1,5},{2,6},{3,7},{4,0},{5,1},{6,2},{7,3},{8,12},{9,13},{10,... | collective-permute-start | bytes 417800 | tf_op jit(solution)/shard_map/ppermute | solution.py:256
  14.5 5.7 %collective-permute-start.5 = (bf16[2,17,16,128]{3,2,1,0:T(8,128)(2,1)S(1)}, bf16[2,17,16,128]{3,2,1,0:T(8,128)(2,1)S(1)}, u32[]{:S(2)}, u32[]{:S(2)}) collective-permute-start(bf16[2,17,16,128]{3,2,1,0:T(8,128)(2,1)S(1)} %collective-permute-done.1.refs_1_), channel_id=1, source_target_pairs={{0,4},{1,5},{2,6},{3,7},{4,0},{5,1},{6,2},{7,3},{8,12},{9,13},{10,... | collective-permute-start | bytes 417800 | tf_op jit(solution)/shard_map/ppermute | solution.py:256
  18.2 1.9 %collective-permute-start.7 = (bf16[17,16,128]{2,1,0:T(8,128)(2,1)S(1)}, bf16[17,16,128]{2,1,0:T(8,128)(2,1)S(1)}, u32[]{:S(2)}, u32[]{:S(2)}) collective-permute-start(bf16[17,16,128]{2,1,0:T(8,128)(2,1)S(1)} %slice_bitcast_fusion), channel_id=1, source_target_pairs={{0,4},{1,5},{2,6},{3,7},{4,0},{5,1},{6,2},{7,3},{8,12},{9,13},{10,... | collective-permute-start | bytes 208904 | tf_op jit(solution)/shard_map/ppermute | solution.py:256
  18.3 1.6 %copy-start = (bf16[8,2,256,256]{3,2,1,0:T(8,128)(2,1)S(1)}, bf16[8,2,256,256]{3,2,1,0:T(8,128)(2,1)}, u32[]{:S(2)}) copy-start(bf16[8,2,256,256]{3,2,1,0:T(8,128)(2,1)} %constant.2.clone.table_ref) | copy-start | bytes 6291460

commit v3 on v2

--- a/solution.py
+++ b/solution.py
@@ -11,22 +11,24 @@
 LANES = 128
 CORES = 2
 NUM_LAGS = 2 * MAXLAG + 1
-PADDED_LAGS = 256
-BEHIND = 0
+BLOCK = 2 * LANES
 VMEM_LIMIT = 32 << 20
 
 
 def lag_table(nbins):
     freq = np.arange(nbins, dtype=np.int64) + 1
-    shift = np.arange(NUM_LAGS, dtype=np.int64) - MAXLAG
+    shift = np.arange(LANES, dtype=np.int64)
     theta = (freq[:, None] * shift[None, :] % (2 * nbins)) * (np.pi / nbins)
-    cosine = (np.cos(theta) / nbins).reshape(nbins // LANES, LANES, NUM_LAGS)
-    sine = (-np.sin(theta) / nbins).reshape(nbins // LANES, LANES, NUM_LAGS)
-    table = np.concatenate([cosine, sine], axis=1).astype(np.float32)
-    table = np.pad(table, ((0, 0), (0, 0), (0, PADDED_LAGS - NUM_LAGS)))
+    used = shift[None, :] <= MAXLAG
+    table = np.stack([np.where(used, turn(theta) / nbins, 0.0) for turn in (np.cos, np.sin)]).astype(np.float32)
     high = table.astype(ml_dtypes.bfloat16)
     low = (table - high.astype(np.float32)).astype(ml_dtypes.bfloat16)
-    return np.stack([high, low], axis=1)
+    pair = np.concatenate([high, low], axis=-1).reshape(2, nbins // BLOCK, BLOCK, 2 * LANES)
+    return pair.transpose(1, 0, 2, 3)
+
+
+def in_hbm(value):
+    return pltpu.with_memory_space_constraint(value, pltpu.HBM)
 
 
 def whiten_kernel(mask_ref, spectra_ref, out_ref):
@@ -66,7 +68,7 @@
         out_specs=pl.BlockSpec(memory_space=pltpu.VMEM),
         compiler_params=pltpu.CompilerParams(vmem_limit_bytes=VMEM_LIMIT),
         name="whiten",
-    )(keep_mask, spectra)
+    )(in_hbm(keep_mask), in_hbm(spectra))
 
 
 def hold_kernel(table_ref, held_ref, arrived):
@@ -86,7 +88,7 @@
         scratch_shapes=[pltpu.SemaphoreType.DMA((table.shape[0],))],
         compiler_params=pltpu.CompilerParams(vmem_limit_bytes=VMEM_LIMIT),
         name="hold",
-    )(table)
+    )(in_hbm(table))
 
 
 def exchange_plan(groups):
@@ -152,45 +154,48 @@
                 pattern_ref[slot, fb, 2 * duo] = jnp.where(upper, tile, turned)
                 pattern_ref[slot, fb, 2 * duo + 1] = jnp.where(upper, turned, tile)
 
-    crosses = []
-
-    def transform(fb):
-        cross = crosses[fb]
+    def transform(cross, part, p):
         size = cross.shape[0]
         top = cross.astype(jnp.bfloat16)
         rest = (cross - top.astype(jnp.float32)).astype(jnp.bfloat16)
-        both = jnp.dot(jnp.concatenate([top, rest], axis=0), held_ref[fb, 0], preferred_element_type=jnp.float32)
-        return both[:size] + both[size:] + jnp.dot(top, held_ref[fb, 1], preferred_element_type=jnp.float32)
-
-    total = jnp.zeros((channels * 2 * duos * rows, PADDED_LAGS), jnp.float32)
-    for fb in range(half):
+        both = jnp.dot(jnp.concatenate([top, rest], axis=0), held_ref[p, part], preferred_element_type=jnp.float32)
+        return both[:size, :LANES] + (both[:size, LANES:] + both[size:, :LANES])
+
+    cosines = sines = None
+    for p in range(half * LANES // BLOCK):
         lines = {}
-        for side in range(2):
-            acc = {}
-            for n, (k, load) in enumerate(far_loads[side]):
-                far_re = load(fb)
-                far_im = load(half + fb)
-                for i in range(channels):
-                    near_re = pattern_ref[k, fb, i]
-                    near_im = pattern_ref[k, half + fb, i]
-                    for duo in range(duos):
-                        fr = far_re[duo * rows : (duo + 1) * rows]
-                        fi = far_im[duo * rows : (duo + 1) * rows]
-                        re = near_re * fr + near_im * fi
-                        im = near_im * fr - near_re * fi
-                        if n:
-                            re = acc[i, duo][0] + re
-                            im = acc[i, duo][1] + im
-                        acc[i, duo] = (re, im)
-            for (i, duo), (re, im) in acc.items():
-                lines[i, side, duo] = jnp.concatenate([re, im], axis=1)
-        crosses.append(jnp.concatenate([lines[key] for key in sorted(lines)], axis=0))
-        if fb >= BEHIND:
-            total = total + transform(fb - BEHIND)
-    for fb in range(half - BEHIND, half):
-        total = total + transform(fb)
-    for side in range(PADDED_LAGS // LANES):
-        lag_ref[side] = total[:, side * LANES : (side + 1) * LANES]
+        for fb in range(p * BLOCK // LANES, (p + 1) * BLOCK // LANES):
+            for side in range(2):
+                acc = {}
+                for n, (k, load) in enumerate(far_loads[side]):
+                    far_re = load(fb)
+                    far_im = load(half + fb)
+                    for i in range(channels):
+                        near_re = pattern_ref[k, fb, i]
+                        near_im = pattern_ref[k, half + fb, i]
+                        for duo in range(duos):
+                            fr = far_re[duo * rows : (duo + 1) * rows]
+                            fi = far_im[duo * rows : (duo + 1) * rows]
+                            re = near_re * fr + near_im * fi
+                            im = near_im * fr - near_re * fi
+                            if n:
+                                re = acc[i, duo][0] + re
+                                im = acc[i, duo][1] + im
+                            acc[i, duo] = (re, im)
+                for (i, duo), value in acc.items():
+                    lines.setdefault((i, side, duo), []).append(value)
+        for part in range(2):
+            cross = jnp.concatenate(
+                [jnp.concatenate([value[part] for value in lines[key]], axis=1) for key in sorted(lines)], axis=0
+            )
+            if part:
+                sine = transform(cross, part, p)
+            else:
+                cosine = transform(cross, part, p)
+        cosines = cosine if cosines is None else cosines + cosine
+        sines = sine if sines is None else sines + sine
+    lag_ref[0] = cosines
+    lag_ref[1] = sines
 
     counts = {}
     for side in range(2):
@@ -206,11 +211,14 @@
     lines = channels * 2 * channels
     pairs = sum(pair_ref[pl.ds(s, lines, stride=windows), :] for s in range(windows))
     pairs = jnp.maximum(pairs, 1.0)
-    parts = []
-    for side in range(PADDED_LAGS // LANES):
-        lag = sum(lag_ref[side, pl.ds(s, lines, stride=windows), :] for s in range(windows))
-        parts.append(lag / pairs)
-    result = jnp.concatenate(parts, axis=1)
+    cosine = sum(lag_ref[0, pl.ds(s, lines, stride=windows), :] for s in range(windows))
+    sine = sum(lag_ref[1, pl.ds(s, lines, stride=windows), :] for s in range(windows))
+    ahead = (cosine - sine) / pairs
+    behind = (cosine + sine) / pairs
+    lane = lax.broadcasted_iota(jnp.int32, behind.shape, 1)
+    behind = jnp.take_along_axis(behind, jnp.maximum(MAXLAG - lane, 0), axis=1)
+    ahead = pltpu.roll(ahead, MAXLAG, 1)
+    result = jnp.concatenate([jnp.where(lane < MAXLAG, behind, ahead), ahead], axis=1)
     for i in range(channels):
         block = result[i * 2 * channels : (i + 1) * 2 * channels]
         block = jnp.where(core == 0, block, pltpu.roll(block, channels, 0))
@@ -230,7 +238,7 @@
         out_specs=vmem,
         scratch_shapes=[
             pltpu.VMEM((groups, blocks, channels, 2 * windows, LANES), jnp.float32),
-            pltpu.VMEM((PADDED_LAGS // LANES, lines, LANES), jnp.float32),
+            pltpu.VMEM((2, lines, LANES), jnp.float32),
             pltpu.VMEM((lines, LANES), jnp.float32),
         ],
         compiler_params=pltpu.CompilerParams(vmem_limit_bytes=VMEM_LIMIT),

time: 22 us -> 20.3 us (0.923)
  the two profiles are of different devices: /device:TPU:5 before, /device:TPU:0 now
where the time goes in v3:
time: 20.3 us; the launch traced here: 20.1 us
  starting transfers between devices  14.2 us (70%)
  Pallas kernels  3.95 us (19%)
  waiting for transfers between devices  1.93 us (10%)
    ppermute x8, starting transfers between devices, send(): return lax.ppermute(value, ('chan', 'tm'), route(move))  14.2 us
    ppermute x8, waiting for transfers between devices, send(): return lax.ppermute(value, ('chan', 'tm'), route(move))  1.93 us
    pallas_call x1, Pallas kernels, correlate(): pl.pallas_call(kernel, out_shape=jax.ShapeDtypeStruct((channels, 2 * chan...  1.7 us
    pallas_call x1, Pallas kernels, hold(): pl.pallas_call(hold_kernel, out_shape=pltpu.VMEM(table.shape, table.dtype...  1.22 us
    pallas_call x1, Pallas kernels, whiten(): pl.pallas_call(whiten_kernel, out_shape=pltpu.VMEM((width // LANES + 1, c...  1.04 us
  transfers between devices with their start and end apart: 8, of which 2 were waited for; matrix products, arithmetic and copies ran while one was open for 0% of the time, Pallas kernels for 6%

profile of v3, /device:TPU:0, one launch (start us, length us, event | category | flops | bytes accessed | tf_op | source)
XLA Modules:
  0.0 20.1 jit_solution(17225190257323652728)
XLA Ops:
  0.0 1.0 %whiten.1.refs_0_ = bf16[17,16,128]{2,1,0:T(8,128)(2,1)S(1)} custom-call(s32[4,4]{1,0:T(4,128)} %mask_ref.1, f32[4,4,2048]{2,1,0:T(4,128)} %spectra_ref.1), custom_call_target="tpu_custom_call" | custom-call | tf_op jit(solution)/shard_map/whiten/pallas_call | solution.py:64
  1.0 0.5 %collective-permute-start = (bf16[17,16,128]{2,1,0:T(8,128)(2,1)S(1)}, bf16[17,16,128]{2,1,0:T(8,128)(2,1)S(1)}, u32[]{:S(2)}, u32[]{:S(2)}) collective-permute-start(bf16[17,16,128]{2,1,0:T(8,128)(2,1)S(1)} %whiten.1.refs_0_), channel_id=1, source_target_pairs={{0,4},{1,5},{2,6},{3,7},{4,0},{5,1},{6,2},{7,3},{8,12},{9,13},{10,... | collective-permute-start | bytes 208904 | tf_op jit(solution)/shard_map/ppermute | solution.py:264
  1.6 0.9 %collective-permute-done = bf16[17,16,128]{2,1,0:T(8,128)(2,1)S(1)} collective-permute-done((bf16[17,16,128]{2,1,0:T(8,128)(2,1)S(1)}, bf16[17,16,128]{2,1,0:T(8,128)(2,1)S(1)}, u32[]{:S(2)}, u32[]{:S(2)}) %collective-permute-start) | collective-permute-done | bytes 69664 | tf_op jit(solution)/shard_map/ppermute | solution.py:264
  2.5 3.0 %collective-permute-start.2 = (bf16[2,17,16,128]{3,2,1,0:T(8,128)(2,1)S(1)}, bf16[2,17,16,128]{3,2,1,0:T(8,128)(2,1)S(1)}, u32[]{:S(2)}, u32[]{:S(2)}) collective-permute-start(bf16[2,17,16,128]{3,2,1,0:T(8,128)(2,1)S(1)} %pad_maximum_fusion), channel_id=1, source_target_pairs={{0,8},{1,0},{2,24},{3,16},{4,20},{5,28},{6,4},{7,12},{8,9},{9,1},{... | collective-permute-start | bytes 417800 | tf_op jit(solution)/shard_map/ppermute | solution.py:264
  5.5 0.7 %collective-permute-start.1 = (bf16[2,17,16,128]{3,2,1,0:T(8,128)(2,1)S(1)}, bf16[2,17,16,128]{3,2,1,0:T(8,128)(2,1)S(1)}, u32[]{:S(2)}, u32[]{:S(2)}) collective-permute-start(bf16[2,17,16,128]{3,2,1,0:T(8,128)(2,1)S(1)} %pad_maximum_fusion), channel_id=1, source_target_pairs={{0,0},{1,8},{2,16},{3,24},{4,28},{5,20},{6,12},{7,4},{8,1},{9,9},{... | collective-permute-start | bytes 417800 | tf_op jit(solution)/shard_map/ppermute | solution.py:264
  6.1 4.3 %collective-permute-start.3 = (bf16[2,17,16,128]{3,2,1,0:T(8,128)(2,1)S(1)}, bf16[2,17,16,128]{3,2,1,0:T(8,128)(2,1)S(1)}, u32[]{:S(2)}, u32[]{:S(2)}) collective-permute-start(bf16[2,17,16,128]{3,2,1,0:T(8,128)(2,1)S(1)} %pad_maximum_fusion), channel_id=1, source_target_pairs={{0,1},{1,0},{2,3},{3,2},{4,6},{5,7},{6,4},{7,5},{8,9},{9,8},{10,11... | collective-permute-start | bytes 417800 | tf_op jit(solution)/shard_map/ppermute | solution.py:264
  10.4 3.7 %collective-permute-start.4 = (bf16[17,16,128]{2,1,0:T(8,128)(2,1)S(1)}, bf16[17,16,128]{2,1,0:T(8,128)(2,1)S(1)}, u32[]{:S(2)}, u32[]{:S(2)}) collective-permute-start(bf16[17,16,128]{2,1,0:T(8,128)(2,1)S(1)} %whiten.1.refs_0_), channel_id=1, source_target_pairs={{0,3},{1,2},{2,1},{3,0},{4,7},{5,6},{6,5},{7,4},{8,11},{9,10},{10,... | collective-permute-start | bytes 208904 | tf_op jit(solution)/shard_map/ppermute | solution.py:264
  14.1 0.0 collective-permute-done.2.refs_2_
  14.1 0.0 collective-permute-start.6
  14.1 0.0 collective-permute-done.1.refs_1_
  14.1 0.5 %collective-permute-start.5 = (bf16[2,17,16,128]{3,2,1,0:T(8,128)(2,1)S(1)}, bf16[2,17,16,128]{3,2,1,0:T(8,128)(2,1)S(1)}, u32[]{:S(2)}, u32[]{:S(2)}) collective-permute-start(bf16[2,17,16,128]{3,2,1,0:T(8,128)(2,1)S(1)} %collective-permute-done.1.refs_1_), channel_id=1, source_target_pairs={{0,4},{1,5},{2,6},{3,7},{4,0},{5,1},{6,2},{7,3},{8,12},{9,13},{10,... | collective-permute-start | bytes 417800 | tf_op jit(solution)/shard_map/ppermute | solution.py:264
  14.6 0.0 collective-permute-done.3.refs_3_
  14.6 1.5 %collective-permute-start.7 = (bf16[17,16,128]{2,1,0:T(8,128)(2,1)S(1)}, bf16[17,16,128]{2,1,0:T(8,128)(2,1)S(1)}, u32[]{:S(2)}, u32[]{:S(2)}) collective-permute-start(bf16[17,16,128]{2,1,0:T(8,128)(2,1)S(1)} %slice_bitcast_fusion), channel_id=1, source_target_pairs={{0,4},{1,5},{2,6},{3,7},{4,0},{5,1},{6,2},{7,3},{8,12},{9,13},{10,... | collective-permute-start | bytes 208904 | tf_op jit(solution)/shard_map/ppermute | solution.py:264
  16.2 1.2 %hold.1.refs_8_ = bf16[4,2,256,256]{3,2,1,0:T(8,128)(2,1)S(1)} custom-call(bf16[4,2,256,256]{3,2,1,0:T(8,128)(2,1)} %constant.2.clone.table_ref), custom_call_target="tpu_custom_call" | custom-call | tf_op jit(solution)/shard_map/hold/pallas_call | solution.py:83
  17.4 1.0 %collective-permute-done.4.refs_4_ = bf16[17,16,128]{2,1,0:T(8,128)(2,1)S(1)} collective-permute-done((bf16[17,16,128]{2,1,0:T(8,128)(2,1)S(1)}, bf16[17,16,128]{2,1,0:T(8,128)(2,1)S(1)}, u32[]{:S(2)}, u32[]{:S(2)}) %collective-permute-start.4) | collective-permute-done | bytes 69664 | tf_op jit(solution)/shard_map/ppermute | solution.py:264
  18.4 0.0 collective-permute-done.7.refs_7_
  18.4 0.0 collective-permute-done.6.refs_6_
  18.4 0.0 collective-permute-done.5.refs_5_
  18.4 1.7 %correlate.1 = f32[4,8,201]{2,1,0:T(8,128)} custom-call(bf16[17,16,128]{2,1,0:T(8,128)(2,1)S(1)} %whiten.1.refs_0_, bf16[2,17,16,128]{3,2,1,0:T(8,128)(2,1)S(1)} %collective-permute-done.1.refs_1_, bf16[2,17,16,128]{3,2,1,0:T(8,128)(2,1)S(1)} %collective-permute-done.2.refs_2_, bf16[2,17,16,128]{3,2,1,0:T(8,128)(2,1)S(1)} %collective-permute-done.3.refs_3_, ...), custom_call_target="tpu_custom_call" | custom-call | tf_op jit(solution)/shard_map/correlate/pallas_call | solution.py:234
  (2 shorter events, 0.0 us)
Async XLA Ops:
  1.0 1.4 %collective-permute-start = (bf16[17,16,128]{2,1,0:T(8,128)(2,1)S(1)}, bf16[17,16,128]{2,1,0:T(8,128)(2,1)S(1)}, u32[]{:S(2)}, u32[]{:S(2)}) collective-permute-start(bf16[17,16,128]{2,1,0:T(8,128)(2,1)S(1)} %whiten.1.refs_0_), channel_id=1, source_target_pairs={{0,4},{1,5},{2,6},{3,7},{4,0},{5,1},{6,2},{7,3},{8,12},{9,13},{10,... | collective-permute-start | bytes 208904 | tf_op jit(solution)/shard_map/ppermute | solution.py:264
  2.5 11.6 %collective-permute-start.2 = (bf16[2,17,16,128]{3,2,1,0:T(8,128)(2,1)S(1)}, bf16[2,17,16,128]{3,2,1,0:T(8,128)(2,1)S(1)}, u32[]{:S(2)}, u32[]{:S(2)}) collective-permute-start(bf16[2,17,16,128]{3,2,1,0:T(8,128)(2,1)S(1)} %pad_maximum_fusion), channel_id=1, source_target_pairs={{0,8},{1,0},{2,24},{3,16},{4,20},{5,28},{6,4},{7,12},{8,9},{9,1},{... | collective-permute-start | bytes 417800 | tf_op jit(solution)/shard_map/ppermute | solution.py:264
  5.5 8.7 %collective-permute-start.1 = (bf16[2,17,16,128]{3,2,1,0:T(8,128)(2,1)S(1)}, bf16[2,17,16,128]{3,2,1,0:T(8,128)(2,1)S(1)}, u32[]{:S(2)}, u32[]{:S(2)}) collective-permute-start(bf16[2,17,16,128]{3,2,1,0:T(8,128)(2,1)S(1)} %pad_maximum_fusion), channel_id=1, source_target_pairs={{0,0},{1,8},{2,16},{3,24},{4,28},{5,20},{6,12},{7,4},{8,1},{9,9},{... | collective-permute-start | bytes 417800 | tf_op jit(solution)/shard_map/ppermute | solution.py:264
  6.1 8.5 %collective-permute-start.3 = (bf16[2,17,16,128]{3,2,1,0:T(8,128)(2,1)S(1)}, bf16[2,17,16,128]{3,2,1,0:T(8,128)(2,1)S(1)}, u32[]{:S(2)}, u32[]{:S(2)}) collective-permute-start(bf16[2,17,16,128]{3,2,1,0:T(8,128)(2,1)S(1)} %pad_maximum_fusion), channel_id=1, source_target_pairs={{0,1},{1,0},{2,3},{3,2},{4,6},{5,7},{6,4},{7,5},{8,9},{9,8},{10,11... | collective-permute-start | bytes 417800 | tf_op jit(solution)/shard_map/ppermute | solution.py:264
  10.4 8.0 %collective-permute-start.4 = (bf16[17,16,128]{2,1,0:T(8,128)(2,1)S(1)}, bf16[17,16,128]{2,1,0:T(8,128)(2,1)S(1)}, u32[]{:S(2)}, u32[]{:S(2)}) collective-permute-start(bf16[17,16,128]{2,1,0:T(8,128)(2,1)S(1)} %whiten.1.refs_0_), channel_id=1, source_target_pairs={{0,3},{1,2},{2,1},{3,0},{4,7},{5,6},{6,5},{7,4},{8,11},{9,10},{10,... | collective-permute-start | bytes 208904 | tf_op jit(solution)/shard_map/ppermute | solution.py:264
  14.1 4.3 %collective-permute-start.6 = (bf16[2,17,16,128]{3,2,1,0:T(8,128)(2,1)S(1)}, bf16[2,17,16,128]{3,2,1,0:T(8,128)(2,1)S(1)}, u32[]{:S(2)}, u32[]{:S(2)}) collective-permute-start(bf16[2,17,16,128]{3,2,1,0:T(8,128)(2,1)S(1)} %collective-permute-done.2.refs_2_), channel_id=1, source_target_pairs={{0,4},{1,5},{2,6},{3,7},{4,0},{5,1},{6,2},{7,3},{8,12},{9,13},{10,... | collective-permute-start | bytes 417800 | tf_op jit(solution)/shard_map/ppermute | solution.py:264
  14.1 4.3 %collective-permute-start.5 = (bf16[2,17,16,128]{3,2,1,0:T(8,128)(2,1)S(1)}, bf16[2,17,16,128]{3,2,1,0:T(8,128)(2,1)S(1)}, u32[]{:S(2)}, u32[]{:S(2)}) collective-permute-start(bf16[2,17,16,128]{3,2,1,0:T(8,128)(2,1)S(1)} %collective-permute-done.1.refs_1_), channel_id=1, source_target_pairs={{0,4},{1,5},{2,6},{3,7},{4,0},{5,1},{6,2},{7,3},{8,12},{9,13},{10,... | collective-permute-start | bytes 417800 | tf_op jit(solution)/shard_map/ppermute | solution.py:264
  14.6 3.8 %collective-permute-start.7 = (bf16[17,16,128]{2,1,0:T(8,128)(2,1)S(1)}, bf16[17,16,128]{2,1,0:T(8,128)(2,1)S(1)}, u32[]{:S(2)}, u32[]{:S(2)}) collective-permute-start(bf16[17,16,128]{2,1,0:T(8,128)(2,1)S(1)} %slice_bitcast_fusion), channel_id=1, source_target_pairs={{0,4},{1,5},{2,6},{3,7},{4,0},{5,1},{6,2},{7,3},{8,12},{9,13},{10,... | collective-permute-start | bytes 208904 | tf_op jit(solution)/shard_map/ppermute | solution.py:264

commit v4 on v3

--- a/solution.py
+++ b/solution.py
@@ -31,17 +31,17 @@
     return pltpu.with_memory_space_constraint(value, pltpu.HBM)
 
 
-def whiten_kernel(mask_ref, spectra_ref, out_ref):
+def whiten_into(out_ref, spectra_ref, mask_ref):
     channels, windows, width = spectra_ref.shape
     nbins = width // 2
     blocks = width // LANES
-    row = lax.broadcasted_iota(jnp.int32, (windows, 1), 0)
+    shape = (windows, windows)
+    diagonal = lax.broadcasted_iota(jnp.int32, shape, 0) == lax.broadcasted_iota(jnp.int32, shape, 1)
     pieces = []
     masks = []
     for ch in range(channels):
-        keep = jnp.zeros((windows, 1), jnp.float32)
-        for s in range(windows):
-            keep = jnp.where(row == s, mask_ref[ch, s].astype(jnp.float32), keep)
+        keep = jnp.broadcast_to(mask_ref[ch : ch + 1].astype(jnp.float32), shape)
+        keep = jnp.sum(jnp.where(diagonal, keep, 0.0), axis=1, keepdims=True)
         spec = spectra_ref[ch]
         re = spec[:, :nbins]
         im = spec[:, nbins:]
@@ -59,36 +59,57 @@
     out_ref[blocks] = jnp.concatenate(masks, axis=0).astype(jnp.bfloat16)
 
 
-def whiten(spectra, keep_mask):
+def whiten_kernel(spectra_ref, mask_ref, table_ref, out_ref, held_ref, near_ref, kept_ref, arrived):
+    spectra = pltpu.make_async_copy(spectra_ref, near_ref, arrived.at[0])
+    table = pltpu.make_async_copy(table_ref, held_ref, arrived.at[1])
+    mask = pltpu.make_async_copy(mask_ref, kept_ref, arrived.at[2])
+    spectra.start()
+    mask.start()
+    table.start()
+    mask.wait()
+    spectra.wait()
+    whiten_into(out_ref, near_ref, kept_ref)
+    table.wait()
+
+
+def whiten(spectra, keep_mask, table):
     channels, windows, width = spectra.shape
+    vmem = pl.BlockSpec(memory_space=pltpu.VMEM)
+    anywhere = pl.BlockSpec(memory_space=pl.ANY)
     return pl.pallas_call(
         whiten_kernel,
-        out_shape=pltpu.VMEM((width // LANES + 1, channels * windows, LANES), jnp.bfloat16),
-        in_specs=[pl.BlockSpec(memory_space=pltpu.SMEM), pl.BlockSpec(memory_space=pltpu.VMEM)],
-        out_specs=pl.BlockSpec(memory_space=pltpu.VMEM),
+        out_shape=(
+            pltpu.VMEM((width // LANES + 1, channels * windows, LANES), jnp.bfloat16),
+            pltpu.VMEM(table.shape, table.dtype),
+        ),
+        in_specs=[anywhere] * 3,
+        out_specs=(vmem, vmem),
+        scratch_shapes=[
+            pltpu.VMEM(spectra.shape, spectra.dtype),
+            pltpu.VMEM(keep_mask.shape, keep_mask.dtype),
+            pltpu.SemaphoreType.DMA((3,)),
+        ],
         compiler_params=pltpu.CompilerParams(vmem_limit_bytes=VMEM_LIMIT),
         name="whiten",
-    )(in_hbm(keep_mask), in_hbm(spectra))
-
-
-def hold_kernel(table_ref, held_ref, arrived):
-    fetches = [pltpu.make_async_copy(table_ref.at[n], held_ref.at[n], arrived.at[n]) for n in range(table_ref.shape[0])]
-    for fetch in fetches:
-        fetch.start()
-    for fetch in fetches:
-        fetch.wait()
-
-
-def hold(table):
+    )(in_hbm(spectra), in_hbm(keep_mask), in_hbm(table))
+
+
+def join_kernel(own_ref, spectra_ref, mask_ref, out_ref):
+    out_ref[0] = own_ref[...]
+    whiten_into(out_ref.at[1], spectra_ref, mask_ref)
+
+
+def join(own, spectra, keep_mask):
+    vmem = pl.BlockSpec(memory_space=pltpu.VMEM)
+    held = [pltpu.with_memory_space_constraint(value, pltpu.VMEM) for value in (own, spectra, keep_mask)]
     return pl.pallas_call(
-        hold_kernel,
-        out_shape=pltpu.VMEM(table.shape, table.dtype),
-        in_specs=[pl.BlockSpec(memory_space=pl.ANY)],
-        out_specs=pl.BlockSpec(memory_space=pltpu.VMEM),
-        scratch_shapes=[pltpu.SemaphoreType.DMA((table.shape[0],))],
+        join_kernel,
+        out_shape=pltpu.VMEM((2, *own.shape), own.dtype),
+        in_specs=[vmem] * 3,
+        out_specs=vmem,
         compiler_params=pltpu.CompilerParams(vmem_limit_bytes=VMEM_LIMIT),
-        name="hold",
-    )(in_hbm(table))
+        name="join",
+    )(*held)
 
 
 def exchange_plan(groups):
@@ -107,7 +128,7 @@
     take = lambda count: [refs.pop(0) for _ in range(count)]
     (own_ref,), direct_refs = take(1), take(len(plan))
     passed_refs = {n: refs.pop(0) for n in range(len(plan)) if passes(plan[n])}
-    held_ref, out_ref, pattern_ref, lag_ref, pair_ref = refs
+    held_ref, out_ref, pattern_ref, cross_ref, pair_ref = refs
     blocks = own_ref.shape[0] - 1
     half = blocks // 2
     duos = channels // 2
@@ -161,10 +182,11 @@
         both = jnp.dot(jnp.concatenate([top, rest], axis=0), held_ref[p, part], preferred_element_type=jnp.float32)
         return both[:size, :LANES] + (both[:size, LANES:] + both[size:, :LANES])
 
-    cosines = sines = None
+    lines = channels * 2 * channels
+    cosine = sine = None
     for p in range(half * LANES // BLOCK):
-        lines = {}
-        for fb in range(p * BLOCK // LANES, (p + 1) * BLOCK // LANES):
+        span = range(p * BLOCK // LANES, (p + 1) * BLOCK // LANES)
+        for fb in span:
             for side in range(2):
                 acc = {}
                 for n, (k, load) in enumerate(far_loads[side]):
@@ -183,19 +205,17 @@
                                 im = acc[i, duo][1] + im
                             acc[i, duo] = (re, im)
                 for (i, duo), value in acc.items():
-                    lines.setdefault((i, side, duo), []).append(value)
+                    row = ((i * 2 + side) * duos + duo) * rows
+                    for part in range(2):
+                        cross_ref[part, fb, row : row + rows] = value[part]
+        sums = []
         for part in range(2):
-            cross = jnp.concatenate(
-                [jnp.concatenate([value[part] for value in lines[key]], axis=1) for key in sorted(lines)], axis=0
-            )
-            if part:
-                sine = transform(cross, part, p)
-            else:
-                cosine = transform(cross, part, p)
-        cosines = cosine if cosines is None else cosines + cosine
-        sines = sine if sines is None else sines + sine
-    lag_ref[0] = cosines
-    lag_ref[1] = sines
+            cross = [
+                sum(cross_ref[part, fb, pl.ds(s, lines, stride=windows), :] for s in range(windows)) for fb in span
+            ]
+            sums.append(transform(jnp.concatenate(cross, axis=1), part, p))
+        cosine = sums[0] if p == 0 else cosine + sums[0]
+        sine = sums[1] if p == 0 else sine + sums[1]
 
     counts = {}
     for side in range(2):
@@ -208,11 +228,8 @@
                     counts[i, side, duo] = counts[i, side, duo] + count if n else count
     pair_ref[...] = jnp.concatenate([counts[key] for key in sorted(counts)], axis=0)
 
-    lines = channels * 2 * channels
     pairs = sum(pair_ref[pl.ds(s, lines, stride=windows), :] for s in range(windows))
     pairs = jnp.maximum(pairs, 1.0)
-    cosine = sum(lag_ref[0, pl.ds(s, lines, stride=windows), :] for s in range(windows))
-    sine = sum(lag_ref[1, pl.ds(s, lines, stride=windows), :] for s in range(windows))
     ahead = (cosine - sine) / pairs
     behind = (cosine + sine) / pairs
     lane = lax.broadcasted_iota(jnp.int32, behind.shape, 1)
@@ -238,7 +255,7 @@
         out_specs=vmem,
         scratch_shapes=[
             pltpu.VMEM((groups, blocks, channels, 2 * windows, LANES), jnp.float32),
-            pltpu.VMEM((2, lines, LANES), jnp.float32),
+            pltpu.VMEM((2, blocks // 2, lines, LANES), jnp.float32),
             pltpu.VMEM((lines, LANES), jnp.float32),
         ],
         compiler_params=pltpu.CompilerParams(vmem_limit_bytes=VMEM_LIMIT),
@@ -279,8 +296,9 @@
 
             return send(value, move)
 
-        own = whiten(spectra, keep_mask)
-        chip = jnp.stack([own, swap(own)])
+        sibling = swap(spectra), swap(keep_mask)
+        own, table = whiten(spectra, keep_mask, jnp.asarray(lag_table(width // 2)))
+        chip = join(own, *sibling)
         plan = exchange_plan(groups)
         direct = [fetch(own if blocks[0] == blocks[1] else chip, *blocks) for blocks in plan]
         passed = []
@@ -288,7 +306,6 @@
             if passes(blocks):
                 half = blocks[0] != blocks[1] and blocks[0][0] == "near"
                 passed.append(swap(value[1] if half else value))
-        table = hold(jnp.asarray(lag_table(width // 2)))
         received = (own, *direct, *passed)
         return correlate(groups, received, channels, windows, table)
 

time: 20.3 us -> 19.7 us (0.970)
  Pallas kernels: 3.95 us -> 3.08 us
    pallas_call x2, Pallas kernels: 2.26 us -> 1.47 us  [the longest x1 1.34 us: whiten(): pl.pallas_call(whiten_kernel, out_shape=(pltpu.VMEM((width // LANES + 1,...]
    ppermute x8 -> x9, starting transfers between devices: 14.2 us -> 14.3 us  [send(): return lax.ppermute(value, ('chan', 'tm'), route(move))]
    ppermute x8 -> x9, waiting for transfers between devices: 1.93 us -> 2.04 us  [send(): return lax.ppermute(value, ('chan', 'tm'), route(move))]
  transfers between devices with their start and end apart: 8 -> 9, of which waited for: 2 -> 1; matrix products, arithmetic and copies ran while one was open for 0% -> 0% of each run, Pallas kernels for 6% -> 7%
where the time goes in v4:
time: 19.7 us; the launch traced here: 19.5 us
  starting transfers between devices  14.3 us (73%)
  Pallas kernels  3.08 us (16%)
  waiting for transfers between devices  2.04 us (10%)
    ppermute x9, starting transfers between devices, send(): return lax.ppermute(value, ('chan', 'tm'), route(move))  14.3 us
    ppermute x9, waiting for transfers between devices, send(): return lax.ppermute(value, ('chan', 'tm'), route(move))  2.04 us
    pallas_call x1, Pallas kernels, correlate(): pl.pallas_call(kernel, out_shape=jax.ShapeDtypeStruct((channels, 2 * chan...  1.61 us
    pallas_call x1, Pallas kernels, whiten(): pl.pallas_call(whiten_kernel, out_shape=(pltpu.VMEM((width // LANES + 1,...  1.34 us
  transfers between devices with their start and end apart: 9, of which 1 were waited for; matrix products, arithmetic and copies ran while one was open for 0% of the time, Pallas kernels for 7%

profile of v4, /device:TPU:0, one launch (start us, length us, event | category | flops | bytes accessed | tf_op | source)
XLA Modules:
  0.0 19.5 jit_solution(16479417346966684617)
XLA Ops:
  0.0 0.5 %collective-permute-start = (f32[4,4,2048]{2,1,0:T(4,128)}, f32[4,4,2048]{2,1,0:T(4,128)S(1)}, u32[]{:S(2)}, u32[]{:S(2)}) collective-permute-start(f32[4,4,2048]{2,1,0:T(4,128)} %spectra_ref.1), channel_id=1, source_target_pairs={{0,4},{1,5},{2,6},{3,7},{4,0},{5,1},{6,2},{7,3},{8,12},{9,13},{10,... | collective-permute-start | bytes 393224 | tf_op jit(solution)/shard_map/ppermute | solution.py:281
  0.5 0.1 collective-permute-start.1
  0.5 1.3 %whiten.1 = (bf16[17,16,128]{2,1,0:T(8,128)(2,1)S(1)}, bf16[4,2,256,256]{3,2,1,0:T(8,128)(2,1)S(1)}) custom-call(f32[4,4,2048]{2,1,0:T(4,128)} %spectra_ref.1, s32[4,4]{1,0:T(4,128)} %mask_ref.1, bf16[4,2,256,256]{3,2,1,0:T(8,128)(2,1)} %constant.2.clone.table_ref), custom_call_target="tpu_custom_call" | custom-call | tf_op jit(solution)/shard_map/whiten/pallas_call | solution.py:79
  1.9 0.0 collective-permute-done.1.mask_ref
  1.9 0.0 collective-permute-done.spectra_ref
  1.9 0.1 join.1
  2.0 3.1 %collective-permute-start.3 = (bf16[2,17,16,128]{3,2,1,0:T(8,128)(2,1)S(1)}, bf16[2,17,16,128]{3,2,1,0:T(8,128)(2,1)S(1)}, u32[]{:S(2)}, u32[]{:S(2)}) collective-permute-start(bf16[2,17,16,128]{3,2,1,0:T(8,128)(2,1)S(1)} %join.1), channel_id=1, source_target_pairs={{0,8},{1,0},{2,24},{3,16},{4,20},{5,28},{6,4},{7,12},{8,9},{9,1},{... | collective-permute-start | bytes 417800 | tf_op jit(solution)/shard_map/ppermute | solution.py:281
  5.1 0.7 %collective-permute-start.2 = (bf16[2,17,16,128]{3,2,1,0:T(8,128)(2,1)S(1)}, bf16[2,17,16,128]{3,2,1,0:T(8,128)(2,1)S(1)}, u32[]{:S(2)}, u32[]{:S(2)}) collective-permute-start(bf16[2,17,16,128]{3,2,1,0:T(8,128)(2,1)S(1)} %join.1), channel_id=1, source_target_pairs={{0,0},{1,8},{2,16},{3,24},{4,28},{5,20},{6,12},{7,4},{8,1},{9,9},{... | collective-permute-start | bytes 417800 | tf_op jit(solution)/shard_map/ppermute | solution.py:281
  5.8 4.3 %collective-permute-start.4 = (bf16[2,17,16,128]{3,2,1,0:T(8,128)(2,1)S(1)}, bf16[2,17,16,128]{3,2,1,0:T(8,128)(2,1)S(1)}, u32[]{:S(2)}, u32[]{:S(2)}) collective-permute-start(bf16[2,17,16,128]{3,2,1,0:T(8,128)(2,1)S(1)} %join.1), channel_id=1, source_target_pairs={{0,1},{1,0},{2,3},{3,2},{4,6},{5,7},{6,4},{7,5},{8,9},{9,8},{10,11... | collective-permute-start | bytes 417800 | tf_op jit(solution)/shard_map/ppermute | solution.py:281
  10.0 3.7 %collective-permute-start.5 = (bf16[17,16,128]{2,1,0:T(8,128)(2,1)S(1)}, bf16[17,16,128]{2,1,0:T(8,128)(2,1)S(1)}, u32[]{:S(2)}, u32[]{:S(2)}) collective-permute-start(bf16[17,16,128]{2,1,0:T(8,128)(2,1)S(1)} %get-tuple-element.7.own_ref.refs_0_), channel_id=1, source_target_pairs={{0,3},{1,2},{2,1},{3,0},{4,7},{5,6},{6,5},{7,4},{8,11},{9,10},{10,... | collective-permute-start | bytes 208904 | tf_op jit(solution)/shard_map/ppermute | solution.py:281
  13.7 0.0 collective-permute-done.3.refs_2_
  13.7 0.0 collective-permute-start.7
  13.8 0.0 collective-permute-done.2.refs_1_
  13.8 0.5 %collective-permute-start.6 = (bf16[2,17,16,128]{3,2,1,0:T(8,128)(2,1)S(1)}, bf16[2,17,16,128]{3,2,1,0:T(8,128)(2,1)S(1)}, u32[]{:S(2)}, u32[]{:S(2)}) collective-permute-start(bf16[2,17,16,128]{3,2,1,0:T(8,128)(2,1)S(1)} %collective-permute-done.2.refs_1_), channel_id=1, source_target_pairs={{0,4},{1,5},{2,6},{3,7},{4,0},{5,1},{6,2},{7,3},{8,12},{9,13},{10,... | collective-permute-start | bytes 417800 | tf_op jit(solution)/shard_map/ppermute | solution.py:281
  14.3 0.0 collective-permute-done.4.refs_3_
  14.3 1.5 %collective-permute-start.8 = (bf16[17,16,128]{2,1,0:T(8,128)(2,1)S(1)}, bf16[17,16,128]{2,1,0:T(8,128)(2,1)S(1)}, u32[]{:S(2)}, u32[]{:S(2)}) collective-permute-start(bf16[17,16,128]{2,1,0:T(8,128)(2,1)S(1)} %slice_bitcast_fusion), channel_id=1, source_target_pairs={{0,4},{1,5},{2,6},{3,7},{4,0},{5,1},{6,2},{7,3},{8,12},{9,13},{10,... | collective-permute-start | bytes 208904 | tf_op jit(solution)/shard_map/ppermute | solution.py:281
  15.8 2.0 %collective-permute-done.5.refs_4_ = bf16[17,16,128]{2,1,0:T(8,128)(2,1)S(1)} collective-permute-done((bf16[17,16,128]{2,1,0:T(8,128)(2,1)S(1)}, bf16[17,16,128]{2,1,0:T(8,128)(2,1)S(1)}, u32[]{:S(2)}, u32[]{:S(2)}) %collective-permute-start.5) | collective-permute-done | bytes 69664 | tf_op jit(solution)/shard_map/ppermute | solution.py:281
  17.8 0.0 collective-permute-done.8.refs_7_
  17.8 0.0 collective-permute-done.7.refs_6_
  17.8 0.0 collective-permute-done.6.refs_5_
  17.8 1.6 %correlate.1 = f32[4,8,201]{2,1,0:T(8,128)} custom-call(bf16[17,16,128]{2,1,0:T(8,128)(2,1)S(1)} %get-tuple-element.7.own_ref.refs_0_, bf16[2,17,16,128]{3,2,1,0:T(8,128)(2,1)S(1)} %collective-permute-done.2.refs_1_, bf16[2,17,16,128]{3,2,1,0:T(8,128)(2,1)S(1)} %collective-permute-done.3.refs_2_, ...), custom_call_target="tpu_custom_call" | custom-call | tf_op jit(solution)/shard_map/correlate/pallas_call | solution.py:251
  (1 shorter events, 0.0 us)
Async XLA Ops:
  0.0 1.9 %collective-permute-start = (f32[4,4,2048]{2,1,0:T(4,128)}, f32[4,4,2048]{2,1,0:T(4,128)S(1)}, u32[]{:S(2)}, u32[]{:S(2)}) collective-permute-start(f32[4,4,2048]{2,1,0:T(4,128)} %spectra_ref.1), channel_id=1, source_target_pairs={{0,4},{1,5},{2,6},{3,7},{4,0},{5,1},{6,2},{7,3},{8,12},{9,13},{10,... | collective-permute-start | bytes 393224 | tf_op jit(solution)/shard_map/ppermute | solution.py:281
  0.5 1.4 %collective-permute-start.1 = (s32[4,4]{1,0:T(4,128)}, s32[4,4]{1,0:T(4,128)S(1)}, u32[]{:S(2)}, u32[]{:S(2)}) collective-permute-start(s32[4,4]{1,0:T(4,128)} %mask_ref.1), channel_id=1, source_target_pairs={{0,4},{1,5},{2,6},{3,7},{4,0},{5,1},{6,2},{7,3},{8,12},{9,13},{10,... | collective-permute-start | bytes 200 | tf_op jit(solution)/shard_map/ppermute | solution.py:281
  2.0 11.7 %collective-permute-start.3 = (bf16[2,17,16,128]{3,2,1,0:T(8,128)(2,1)S(1)}, bf16[2,17,16,128]{3,2,1,0:T(8,128)(2,1)S(1)}, u32[]{:S(2)}, u32[]{:S(2)}) collective-permute-start(bf16[2,17,16,128]{3,2,1,0:T(8,128)(2,1)S(1)} %join.1), channel_id=1, source_target_pairs={{0,8},{1,0},{2,24},{3,16},{4,20},{5,28},{6,4},{7,12},{8,9},{9,1},{... | collective-permute-start | bytes 417800 | tf_op jit(solution)/shard_map/ppermute | solution.py:281
  5.1 8.7 %collective-permute-start.2 = (bf16[2,17,16,128]{3,2,1,0:T(8,128)(2,1)S(1)}, bf16[2,17,16,128]{3,2,1,0:T(8,128)(2,1)S(1)}, u32[]{:S(2)}, u32[]{:S(2)}) collective-permute-start(bf16[2,17,16,128]{3,2,1,0:T(8,128)(2,1)S(1)} %join.1), channel_id=1, source_target_pairs={{0,0},{1,8},{2,16},{3,24},{4,28},{5,20},{6,12},{7,4},{8,1},{9,9},{... | collective-permute-start | bytes 417800 | tf_op jit(solution)/shard_map/ppermute | solution.py:281
  5.8 8.5 %collective-permute-start.4 = (bf16[2,17,16,128]{3,2,1,0:T(8,128)(2,1)S(1)}, bf16[2,17,16,128]{3,2,1,0:T(8,128)(2,1)S(1)}, u32[]{:S(2)}, u32[]{:S(2)}) collective-permute-start(bf16[2,17,16,128]{3,2,1,0:T(8,128)(2,1)S(1)} %join.1), channel_id=1, source_target_pairs={{0,1},{1,0},{2,3},{3,2},{4,6},{5,7},{6,4},{7,5},{8,9},{9,8},{10,11... | collective-permute-start | bytes 417800 | tf_op jit(solution)/shard_map/ppermute | solution.py:281
  10.0 7.8 %collective-permute-start.5 = (bf16[17,16,128]{2,1,0:T(8,128)(2,1)S(1)}, bf16[17,16,128]{2,1,0:T(8,128)(2,1)S(1)}, u32[]{:S(2)}, u32[]{:S(2)}) collective-permute-start(bf16[17,16,128]{2,1,0:T(8,128)(2,1)S(1)} %get-tuple-element.7.own_ref.refs_0_), channel_id=1, source_target_pairs={{0,3},{1,2},{2,1},{3,0},{4,7},{5,6},{6,5},{7,4},{8,11},{9,10},{10,... | collective-permute-start | bytes 208904 | tf_op jit(solution)/shard_map/ppermute | solution.py:281
  13.7 4.1 %collective-permute-start.7 = (bf16[2,17,16,128]{3,2,1,0:T(8,128)(2,1)S(1)}, bf16[2,17,16,128]{3,2,1,0:T(8,128)(2,1)S(1)}, u32[]{:S(2)}, u32[]{:S(2)}) collective-permute-start(bf16[2,17,16,128]{3,2,1,0:T(8,128)(2,1)S(1)} %collective-permute-done.3.refs_2_), channel_id=1, source_target_pairs={{0,4},{1,5},{2,6},{3,7},{4,0},{5,1},{6,2},{7,3},{8,12},{9,13},{10,... | collective-permute-start | bytes 417800 | tf_op jit(solution)/shard_map/ppermute | solution.py:281
  13.8 4.1 %collective-permute-start.6 = (bf16[2,17,16,128]{3,2,1,0:T(8,128)(2,1)S(1)}, bf16[2,17,16,128]{3,2,1,0:T(8,128)(2,1)S(1)}, u32[]{:S(2)}, u32[]{:S(2)}) collective-permute-start(bf16[2,17,16,128]{3,2,1,0:T(8,128)(2,1)S(1)} %collective-permute-done.2.refs_1_), channel_id=1, source_target_pairs={{0,4},{1,5},{2,6},{3,7},{4,0},{5,1},{6,2},{7,3},{8,12},{9,13},{10,... | collective-permute-start | bytes 417800 | tf_op jit(solution)/shard_map/ppermute | solution.py:281
  14.3 3.6 %collective-permute-start.8 = (bf16[17,16,128]{2,1,0:T(8,128)(2,1)S(1)}, bf16[17,16,128]{2,1,0:T(8,128)(2,1)S(1)}, u32[]{:S(2)}, u32[]{:S(2)}) collective-permute-start(bf16[17,16,128]{2,1,0:T(8,128)(2,1)S(1)} %slice_bitcast_fusion), channel_id=1, source_target_pairs={{0,4},{1,5},{2,6},{3,7},{4,0},{5,1},{6,2},{7,3},{8,12},{9,13},{10,... | collective-permute-start | bytes 208904 | tf_op jit(solution)/shard_map/ppermute | solution.py:281

commit v5 on v4

v5 whole, which is shorter than its diff:
```python
import jax
import jax.numpy as jnp
import ml_dtypes
import numpy as np
from jax import lax
from jax.experimental import pallas as pl
from jax.experimental.pallas import tpu as pltpu
from jax.sharding import PartitionSpec as P

MAXLAG = 100
LANES = 128
CORES = 2
NUM_LAGS = 2 * MAXLAG + 1
BLOCK = 2 * LANES
VMEM_LIMIT = 32 << 20


def lag_table(nbins):
    freq = np.arange(nbins, dtype=np.int64) + 1
    shift = np.arange(LANES, dtype=np.int64)
    theta = (freq[:, None] * shift[None, :] % (2 * nbins)) * (np.pi / nbins)
    used = shift[None, :] <= MAXLAG
    table = np.stack([np.where(used, turn(theta) / nbins, 0.0) for turn in (np.cos, np.sin)]).astype(np.float32)
    high = table.astype(ml_dtypes.bfloat16)
    low = (table - high.astype(np.float32)).astype(ml_dtypes.bfloat16)
    pair = np.concatenate([high, low], axis=-1).reshape(2, nbins // BLOCK, BLOCK, 2 * LANES)
    return pair.transpose(1, 0, 2, 3)


def in_hbm(value):
    return pltpu.with_memory_space_constraint(value, pltpu.HBM)


def whiten_into(out_ref, spectra_ref, mask_ref):
    channels, windows, width = spectra_ref.shape
    nbins = width // 2
    blocks = width // LANES
    shape = (windows, windows)
    diagonal = lax.broadcasted_iota(jnp.int32, shape, 0) == lax.broadcasted_iota(jnp.int32, shape, 1)
    pieces = []
    masks = []
    for ch in range(channels):
        keep = jnp.broadcast_to(mask_ref[ch : ch + 1].astype(jnp.float32), shape)
        keep = jnp.sum(jnp.where(diagonal, keep, 0.0), axis=1, keepdims=True)
        spec = spectra_ref[ch]
        re = spec[:, :nbins]
        im = spec[:, nbins:]
        power = re * re + im * im
        level = jnp.mean(power, axis=-1, keepdims=True) + 1e-06
        factor = lax.rsqrt(power + 0.5 * level)
        pieces.append((re * factor * keep, im * factor * keep))
        masks.append(jnp.broadcast_to(keep, (windows, LANES)))
    re = jnp.concatenate([p[0] for p in pieces], axis=0).astype(jnp.bfloat16)
    im = jnp.concatenate([p[1] for p in pieces], axis=0).astype(jnp.bfloat16)
    half = blocks // 2
    for fb in range(half):
        out_ref[fb] = re[:, fb * LANES : (fb + 1) * LANES]
        out_ref[half + fb] = im[:, fb * LANES : (fb + 1) * LANES]
    out_ref[blocks] = jnp.concatenate(masks, axis=0).astype(jnp.bfloat16)


def whiten_kernel(spectra_ref, mask_ref, table_ref, out_ref, held_ref, near_ref, kept_ref, arrived):
    spectra = pltpu.make_async_copy(spectra_ref, near_ref, arrived.at[0])
    table = pltpu.make_async_copy(table_ref, held_ref, arrived.at[1])
    mask = pltpu.make_async_copy(mask_ref, kept_ref, arrived.at[2])
    spectra.start()
    mask.start()
    table.start()
    mask.wait()
    spectra.wait()
    whiten_into(out_ref, near_ref, kept_ref)
    table.wait()


def whiten(spectra, keep_mask, table):
    channels, windows, width = spectra.shape
    vmem = pl.BlockSpec(memory_space=pltpu.VMEM)
    anywhere = pl.BlockSpec(memory_space=pl.ANY)
    return pl.pallas_call(
        whiten_kernel,
        out_shape=(
            pltpu.VMEM((width // LANES + 1, channels * windows, LANES), jnp.bfloat16),
            pltpu.VMEM(table.shape, table.dtype),
        ),
        in_specs=[anywhere] * 3,
        out_specs=(vmem, vmem),
        scratch_shapes=[
            pltpu.VMEM(spectra.shape, spectra.dtype),
            pltpu.VMEM(keep_mask.shape, keep_mask.dtype),
            pltpu.SemaphoreType.DMA((3,)),
        ],
        compiler_params=pltpu.CompilerParams(vmem_limit_bytes=VMEM_LIMIT),
        name="whiten",
    )(in_hbm(spectra), in_hbm(keep_mask), in_hbm(table))


def join_kernel(own_ref, spectra_ref, mask_ref, out_ref):
    out_ref[0] = own_ref[...]
    whiten_into(out_ref.at[1], spectra_ref, mask_ref)


def join(own, spectra, keep_mask):
    vmem = pl.BlockSpec(memory_space=pltpu.VMEM)
    held = [pltpu.with_memory_space_constraint(value, pltpu.VMEM) for value in (own, spectra, keep_mask)]
    return pl.pallas_call(
        join_kernel,
        out_shape=pltpu.VMEM((2, *own.shape), own.dtype),
        in_specs=[vmem] * 3,
        out_specs=vmem,
        compiler_params=pltpu.CompilerParams(vmem_limit_bytes=VMEM_LIMIT),
        name="join",
    )(*held)


def exchange_plan(groups):
    far = [(("far", b), ("far", groups - 1 - b)) for b in reversed(range(groups // 2))]
    near = [(("near", k), ("near", groups - 1 - k)) for k in range(1, groups // 2)]
    return far + near + [(("near", groups - 1), ("near", groups - 1))]


def place(groups):
    chan = lax.axis_index("chan")
    return lax.rem(chan, CORES), lax.bitwise_xor(lax.div(chan, CORES), lax.axis_index("tm"))


def slots(blocks, core, turn=0):
    mine = core * (blocks[0][1] ^ blocks[1][1])
    return [lax.bitwise_xor(lax.bitwise_xor(mine, block[1]), turn) for block in blocks]


def spread(blocks, pattern_ref):
    _, count, channels, rows, _ = pattern_ref.shape
    upper = lax.broadcasted_iota(jnp.int32, (rows, LANES), 0) < rows // 2
    for n, ref in enumerate(blocks):
        for fb in range(count):
            block = ref[fb].astype(jnp.float32)
            for duo in range(channels // 2):
                tile = block[duo * rows : (duo + 1) * rows]
                turned = pltpu.roll(tile, rows // 2, 0)
                pattern_ref[n, fb, 2 * duo] = jnp.where(upper, tile, turned)
                pattern_ref[n, fb, 2 * duo + 1] = jnp.where(upper, turned, tile)


def tally(slots, far_ref, pattern_ref, cross_ref, pair_ref):
    _, blocks, channels, rows, _ = pattern_ref.shape
    half = blocks // 2
    duos = channels // 2
    for fb in range(half):
        for side in range(2):
            acc = {}
            for n, slot in enumerate(slots):
                far_re = far_ref[slot, side, fb].astype(jnp.float32)
                far_im = far_ref[slot, side, half + fb].astype(jnp.float32)
                for i in range(channels):
                    near_re = pattern_ref[n, fb, i]
                    near_im = pattern_ref[n, half + fb, i]
                    for duo in range(duos):
                        fr = far_re[duo * rows : (duo + 1) * rows]
                        fi = far_im[duo * rows : (duo + 1) * rows]
                        re = near_re * fr + near_im * fi
                        im = near_im * fr - near_re * fi
                        if n:
                            re = acc[i, duo][0] + re
                            im = acc[i, duo][1] + im
                        acc[i, duo] = (re, im)
            for (i, duo), value in acc.items():
                row = ((i * 2 + side) * duos + duo) * rows
                for part in range(2):
                    cross_ref[part, fb, row : row + rows] = value[part]
    for side in range(2):
        acc = {}
        for n, slot in enumerate(slots):
            far = far_ref[slot, side, 2 * half].astype(jnp.float32)
            for i in range(channels):
                near = pattern_ref[n, 2 * half, i]
                for duo in range(duos):
                    count = near * far[duo * rows : (duo + 1) * rows]
                    acc[i, duo] = acc[i, duo] + count if n else count
        for (i, duo), value in acc.items():
            row = ((i * 2 + side) * duos + duo) * rows
            pair_ref[row : row + rows] = value


def over_windows(ref, windows):
    lines = ref.shape[0] // windows
    return sum(ref[pl.ds(s, lines, stride=windows), :] for s in range(windows))


def near_slots(groups, core, own):
    pairs = [slots(blocks, core) for blocks in exchange_plan(groups)[groups // 2 : -1]]
    return [0, *(mine for mine, _ in pairs)] if own else [groups - 1, *(theirs for _, theirs in pairs)]


def gather_kernel(groups, *refs):
    refs = list(refs)
    take = lambda count: [refs.pop(0) for _ in range(count)]
    near_refs, direct_refs, passed_refs = take(groups // 2), take(groups // 2), take(groups // 2)
    far_ref, part_ref, count_ref, pattern_ref, cross_ref, pair_ref = refs
    windows = pattern_ref.shape[3] // 2
    core, turn = place(groups)
    for blocks, direct, passed in zip(exchange_plan(groups), direct_refs, passed_refs):
        mine, theirs = slots(blocks, core, turn)
        for side in range(2):
            far_ref[mine, side] = direct[side]
            far_ref[theirs, side] = passed[1 - side]
    spread([near_refs[0], *(ref.at[0] for ref in near_refs[1:])], pattern_ref)
    tally(near_slots(groups, core, True), far_ref, pattern_ref, cross_ref, pair_ref)
    for part in range(2):
        for fb in range(cross_ref.shape[1]):
            part_ref[part, fb] = over_windows(cross_ref.at[part, fb], windows)
    count_ref[...] = over_windows(pair_ref, windows)


def finish_kernel(groups, *refs):
    late_refs = refs[: groups // 2]
    far_ref, part_ref, count_ref, held_ref, out_ref, pattern_ref, cross_ref, pair_ref = refs[groups // 2 :]
    channels = pattern_ref.shape[2]
    windows = pattern_ref.shape[3] // 2
    core, _ = place(groups)
    spread(late_refs, pattern_ref)
    tally(near_slots(groups, core, False), far_ref, pattern_ref, cross_ref, pair_ref)

    def transform(part, p):
        span = range(p * BLOCK // LANES, (p + 1) * BLOCK // LANES)
        cross = [part_ref[part, fb] + over_windows(cross_ref.at[part, fb], windows) for fb in span]
        cross = jnp.concatenate(cross, axis=1)
        size = cross.shape[0]
        top = cross.astype(jnp.bfloat16)
        rest = (cross - top.astype(jnp.float32)).astype(jnp.bfloat16)
        both = jnp.dot(jnp.concatenate([top, rest], axis=0), held_ref[p, part], preferred_element_type=jnp.float32)
        return both[:size, :LANES] + (both[:size, LANES:] + both[size:, :LANES])

    cosine, sine = [sum(transform(part, p) for p in range(held_ref.shape[0])) for part in range(2)]
    pairs = jnp.maximum(count_ref[...] + over_windows(pair_ref, windows), 1.0)
    ahead = (cosine - sine) / pairs
    behind = (cosine + sine) / pairs
    lane = lax.broadcasted_iota(jnp.int32, behind.shape, 1)
    behind = jnp.take_along_axis(behind, jnp.maximum(MAXLAG - lane, 0), axis=1)
    ahead = pltpu.roll(ahead, MAXLAG, 1)
    result = jnp.concatenate([jnp.where(lane < MAXLAG, behind, ahead), ahead], axis=1)
    for i in range(channels):
        block = result[i * 2 * channels : (i + 1) * 2 * channels]
        block = jnp.where(core == 0, block, pltpu.roll(block, channels, 0))
        out_ref[i] = block[:, :NUM_LAGS]


def correlate(groups, near, far, late, table, channels, windows):
    count = near[0].shape[0]
    lines = channels * 2 * channels
    vmem = pl.BlockSpec(memory_space=pltpu.VMEM)
    hold = lambda values: [pltpu.with_memory_space_constraint(value, pltpu.VMEM) for value in values]
    scratch = [
        pltpu.VMEM((groups // 2, count, channels, 2 * windows, LANES), jnp.float32),
        pltpu.VMEM((2, count // 2, lines * windows, LANES), jnp.float32),
        pltpu.VMEM((lines * windows, LANES), jnp.float32),
    ]
    sums = pl.pallas_call(
        lambda *refs: gather_kernel(groups, *refs),
        out_shape=(
            pltpu.VMEM((groups, 2, *near[0].shape), near[0].dtype),
            pltpu.VMEM((2, count // 2, lines, LANES), jnp.float32),
            pltpu.VMEM((lines, LANES), jnp.float32),
        ),
        in_specs=[vmem] * (len(near) + len(far)),
        out_specs=(vmem, vmem, vmem),
        scratch_shapes=scratch,
        compiler_params=pltpu.CompilerParams(vmem_limit_bytes=VMEM_LIMIT),
        name="gather",
    )(*hold((*near, *far)))
    return pl.pallas_call(
        lambda *refs: finish_kernel(groups, *refs),
        out_shape=jax.ShapeDtypeStruct((channels, 2 * channels, NUM_LAGS), jnp.float32),
        in_specs=[vmem] * (len(late) + 4),
        out_specs=vmem,
        scratch_shapes=scratch,
        compiler_params=pltpu.CompilerParams(vmem_limit_bytes=VMEM_LIMIT),
        name="finish",
    )(*hold((*late, *sums, table)))


def solution(mesh):
    groups = mesh.shape["tm"]
    assert mesh.shape["chan"] == CORES * groups and groups & (groups - 1) == 0

    def route(move):
        pairs = []
        for line in range(groups):
            for core in range(CORES):
                for t in range(groups):
                    to_line, to_core, to_t = move(line, core, t)
                    source = (line * CORES + core) * groups + t
                    pairs.append((source, (to_line * CORES + to_core) * groups + to_t))
        return pairs

    def send(value, move):
        return lax.ppermute(value, ("chan", "tm"), route(move))

    def local(spectra, keep_mask):
        channels, windows, width = spectra.shape
        swap = lambda value: send(value, lambda line, core, t: (line, 1 - core, t))
        moves = {
            "far": lambda line, core, t, b: (t ^ b, core, line),
            "near": lambda line, core, t, k: (line, core, t ^ k),
        }

        def fetch(value, *blocks):
            def move(line, core, t):
                kind, number = blocks[core]
                return moves[kind](line, core, t, number)

            return send(value, move)

        sibling = swap(spectra), swap(keep_mask)
        own, table = whiten(spectra, keep_mask, jnp.asarray(lag_table(width // 2)))
        chip = join(own, *sibling)
        plan = exchange_plan(groups)
        direct = [fetch(own if blocks[0] == blocks[1] else chip, *blocks) for blocks in plan]
        *direct, last = direct
        far, near = direct[: groups // 2], direct[groups // 2 :]
        far_passed = [swap(value) for value in far]
        late = [last, *(swap(value[1]) for value in near)]
        return correlate(groups, (own, *near), (*far, *far_passed), late, table, channels, windows)

    placed = (P("chan", "tm", None), P("chan", "tm"))
    return jax.shard_map(local, mesh=mesh, in_specs=placed, out_specs=P("chan", "tm", None), check_vma=False)
```

time: 19.7 us -> 19.5 us (0.990)
  waiting for transfers between devices: 2.04 us -> 1.63 us
    ppermute x9, waiting for transfers between devices: 2.04 us -> 1.63 us  [send(): return lax.ppermute(value, ('chan', 'tm'), route(move))]
    pallas_call x1 -> x2, Pallas kernels: 1.61 us -> 1.71 us  [the longest x1 1.31 us: correlate(): pl.pallas_call(lambda *refs: finish_kernel(groups, *refs), out_shape=jax....]
  transfers between devices with their start and end apart: 9 -> 9, of which waited for: 1 -> 1; matrix products, arithmetic and copies ran while one was open for 0% -> 0% of each run, Pallas kernels for 7% -> 9%
where the time goes in v5:
time: 19.5 us; the launch traced here: 19.1 us
  starting transfers between devices  14.3 us (73%)
  Pallas kernels  3.18 us (16%)
  waiting for transfers between devices  1.63 us (8%)
    ppermute x9, starting transfers between devices, send(): return lax.ppermute(value, ('chan', 'tm'), route(move))  14.3 us
    ppermute x9, waiting for transfers between devices, send(): return lax.ppermute(value, ('chan', 'tm'), route(move))  1.63 us
    pallas_call x1, Pallas kernels, whiten(): pl.pallas_call(whiten_kernel, out_shape=(pltpu.VMEM((width // LANES + 1,...  1.34 us
    pallas_call x1, Pallas kernels, correlate(): pl.pallas_call(lambda *refs: finish_kernel(groups, *refs), out_shape=jax....  1.31 us
    pallas_call x1, Pallas kernels, correlate(): pl.pallas_call(lambda *refs: gather_kernel(groups, *refs), out_shape=(plt...  0.4 us
  transfers between devices with their start and end apart: 9, of which 1 were waited for; matrix products, arithmetic and copies ran while one was open for 0% of the time, Pallas kernels for 9%

profile of v5, /device:TPU:0, one launch (start us, length us, event | category | flops | bytes accessed | tf_op | source)
XLA Modules:
  0.0 19.1 jit_solution(6080728360131050143)
XLA Ops:
  0.0 0.5 %collective-permute-start.1 = (f32[4,4,2048]{2,1,0:T(4,128)}, f32[4,4,2048]{2,1,0:T(4,128)S(1)}, u32[]{:S(2)}, u32[]{:S(2)}) collective-permute-start(f32[4,4,2048]{2,1,0:T(4,128)} %spectra_ref.1), channel_id=1, source_target_pairs={{0,4},{1,5},{2,6},{3,7},{4,0},{5,1},{6,2},{7,3},{8,12},{9,13},{10,... | collective-permute-start | bytes 393224 | tf_op jit(solution)/shard_map/ppermute | solution.py:296
  0.5 0.1 collective-permute-start.2
  0.5 1.3 %whiten.1 = (bf16[17,16,128]{2,1,0:T(8,128)(2,1)S(1)}, bf16[4,2,256,256]{3,2,1,0:T(8,128)(2,1)S(1)}) custom-call(f32[4,4,2048]{2,1,0:T(4,128)} %spectra_ref.1, s32[4,4]{1,0:T(4,128)} %mask_ref.1, bf16[4,2,256,256]{3,2,1,0:T(8,128)(2,1)} %constant.2.clone.table_ref), custom_call_target="tpu_custom_call" | custom-call | tf_op jit(solution)/shard_map/whiten/pallas_call | solution.py:79
  1.9 0.0 collective-permute-done.2.mask_ref
  1.9 0.0 collective-permute-done.1.spectra_ref
  1.9 0.1 join.1
  2.0 3.1 %collective-permute-start.5 = (bf16[2,17,16,128]{3,2,1,0:T(8,128)(2,1)S(1)}, bf16[2,17,16,128]{3,2,1,0:T(8,128)(2,1)S(1)}, u32[]{:S(2)}, u32[]{:S(2)}) collective-permute-start(bf16[2,17,16,128]{3,2,1,0:T(8,128)(2,1)S(1)} %join.1), channel_id=1, source_target_pairs={{0,8},{1,0},{2,24},{3,16},{4,20},{5,28},{6,4},{7,12},{8,9},{9,1},{... | collective-permute-start | bytes 417800 | tf_op jit(solution)/shard_map/ppermute | solution.py:296
  5.1 0.7 %collective-permute-start.6 = (bf16[2,17,16,128]{3,2,1,0:T(8,128)(2,1)S(1)}, bf16[2,17,16,128]{3,2,1,0:T(8,128)(2,1)S(1)}, u32[]{:S(2)}, u32[]{:S(2)}) collective-permute-start(bf16[2,17,16,128]{3,2,1,0:T(8,128)(2,1)S(1)} %join.1), channel_id=1, source_target_pairs={{0,0},{1,8},{2,16},{3,24},{4,28},{5,20},{6,12},{7,4},{8,1},{9,9},{... | collective-permute-start | bytes 417800 | tf_op jit(solution)/shard_map/ppermute | solution.py:296
  5.8 4.3 %collective-permute-start.3 = (bf16[2,17,16,128]{3,2,1,0:T(8,128)(2,1)S(1)}, bf16[2,17,16,128]{3,2,1,0:T(8,128)(2,1)S(1)}, u32[]{:S(2)}, u32[]{:S(2)}) collective-permute-start(bf16[2,17,16,128]{3,2,1,0:T(8,128)(2,1)S(1)} %join.1), channel_id=1, source_target_pairs={{0,1},{1,0},{2,3},{3,2},{4,6},{5,7},{6,4},{7,5},{8,9},{9,8},{10,11... | collective-permute-start | bytes 417800 | tf_op jit(solution)/shard_map/ppermute | solution.py:296
  10.0 3.7 %collective-permute-start = (bf16[17,16,128]{2,1,0:T(8,128)(2,1)S(1)}, bf16[17,16,128]{2,1,0:T(8,128)(2,1)S(1)}, u32[]{:S(2)}, u32[]{:S(2)}) collective-permute-start(bf16[17,16,128]{2,1,0:T(8,128)(2,1)S(1)} %get-tuple-element.10.own_ref.refs_0_), channel_id=1, source_target_pairs={{0,3},{1,2},{2,1},{3,0},{4,7},{5,6},{6,5},{7,4},{8,11},{9,10},{10,... | collective-permute-start | bytes 208904 | tf_op jit(solution)/shard_map/ppermute | solution.py:296
  13.7 0.0 collective-permute-done.5.refs_2_
  13.7 0.0 collective-permute-start.7
  13.8 0.0 collective-permute-done.6.refs_3_
  13.8 0.5 %collective-permute-start.8 = (bf16[2,17,16,128]{3,2,1,0:T(8,128)(2,1)S(1)}, bf16[2,17,16,128]{3,2,1,0:T(8,128)(2,1)S(1)}, u32[]{:S(2)}, u32[]{:S(2)}) collective-permute-start(bf16[2,17,16,128]{3,2,1,0:T(8,128)(2,1)S(1)} %collective-permute-done.6.refs_3_), channel_id=1, source_target_pairs={{0,4},{1,5},{2,6},{3,7},{4,0},{5,1},{6,2},{7,3},{8,12},{9,13},{10,... | collective-permute-start | bytes 417800 | tf_op jit(solution)/shard_map/ppermute | solution.py:296
  14.3 0.0 collective-permute-done.3.refs_1_
  14.3 1.5 %collective-permute-start.4 = (bf16[17,16,128]{2,1,0:T(8,128)(2,1)S(1)}, bf16[17,16,128]{2,1,0:T(8,128)(2,1)S(1)}, u32[]{:S(2)}, u32[]{:S(2)}) collective-permute-start(bf16[17,16,128]{2,1,0:T(8,128)(2,1)S(1)} %slice_bitcast_fusion), channel_id=1, source_target_pairs={{0,4},{1,5},{2,6},{3,7},{4,0},{5,1},{6,2},{7,3},{8,12},{9,13},{10,... | collective-permute-start | bytes 208904 | tf_op jit(solution)/shard_map/ppermute | solution.py:296
  15.8 0.0 collective-permute-done.7.refs_4_
  15.8 0.0 collective-permute-done.8.refs_5_
  15.8 0.4 %gather.1 = (bf16[4,2,17,16,128]{4,3,2,1,0:T(8,128)(2,1)S(1)}, f32[2,8,32,128]{3,2,1,0:T(8,128)S(1)}, f32[32,128]{1,0:T(8,128)S(1)}) custom-call(bf16[17,16,128]{2,1,0:T(8,128)(2,1)S(1)} %get-tuple-element.10.own_ref.refs_0_, bf16[2,17,16,128]{3,2,1,0:T(8,128)(2,1)S(1)} %collective-permute-done.3.refs_1_, ...), custom_call_target="tpu_custom_call" | custom-call | tf_op jit(solution)/shard_map/gather/pallas_call | solution.py:257
  16.2 1.6 %collective-permute-done.refs_0_ = bf16[17,16,128]{2,1,0:T(8,128)(2,1)S(1)} collective-permute-done((bf16[17,16,128]{2,1,0:T(8,128)(2,1)S(1)}, bf16[17,16,128]{2,1,0:T(8,128)(2,1)S(1)}, u32[]{:S(2)}, u32[]{:S(2)}) %collective-permute-start) | collective-permute-done | bytes 69664 | tf_op jit(solution)/shard_map/ppermute | solution.py:296
  17.8 0.0 collective-permute-done.4.refs_1_
  17.8 1.3 %finish.1 = f32[4,8,201]{2,1,0:T(8,128)} custom-call(bf16[17,16,128]{2,1,0:T(8,128)(2,1)S(1)} %collective-permute-done.refs_0_, bf16[17,16,128]{2,1,0:T(8,128)(2,1)S(1)} %collective-permute-done.4.refs_1_, bf16[4,2,17,16,128]{4,3,2,1,0:T(8,128)(2,1)S(1)} %get-tuple-element.11.refs_2_, f32[2,8,32,128]{3,2,1,0:T(8,128)S(1)} %get-tuple-element.12.refs_3_, ...), custom_call_target="tpu_custom_call" | custom-call | tf_op jit(solution)/shard_map/finish/pallas_call | solution.py:270
  (1 shorter events, 0.0 us)
Async XLA Ops:
  0.0 1.9 %collective-permute-start.1 = (f32[4,4,2048]{2,1,0:T(4,128)}, f32[4,4,2048]{2,1,0:T(4,128)S(1)}, u32[]{:S(2)}, u32[]{:S(2)}) collective-permute-start(f32[4,4,2048]{2,1,0:T(4,128)} %spectra_ref.1), channel_id=1, source_target_pairs={{0,4},{1,5},{2,6},{3,7},{4,0},{5,1},{6,2},{7,3},{8,12},{9,13},{10,... | collective-permute-start | bytes 393224 | tf_op jit(solution)/shard_map/ppermute | solution.py:296
  0.5 1.4 %collective-permute-start.2 = (s32[4,4]{1,0:T(4,128)}, s32[4,4]{1,0:T(4,128)S(1)}, u32[]{:S(2)}, u32[]{:S(2)}) collective-permute-start(s32[4,4]{1,0:T(4,128)} %mask_ref.1), channel_id=1, source_target_pairs={{0,4},{1,5},{2,6},{3,7},{4,0},{5,1},{6,2},{7,3},{8,12},{9,13},{10,... | collective-permute-start | bytes 200 | tf_op jit(solution)/shard_map/ppermute | solution.py:296
  2.0 11.7 %collective-permute-start.5 = (bf16[2,17,16,128]{3,2,1,0:T(8,128)(2,1)S(1)}, bf16[2,17,16,128]{3,2,1,0:T(8,128)(2,1)S(1)}, u32[]{:S(2)}, u32[]{:S(2)}) collective-permute-start(bf16[2,17,16,128]{3,2,1,0:T(8,128)(2,1)S(1)} %join.1), channel_id=1, source_target_pairs={{0,8},{1,0},{2,24},{3,16},{4,20},{5,28},{6,4},{7,12},{8,9},{9,1},{... | collective-permute-start | bytes 417800 | tf_op jit(solution)/shard_map/ppermute | solution.py:296
  5.1 8.7 %collective-permute-start.6 = (bf16[2,17,16,128]{3,2,1,0:T(8,128)(2,1)S(1)}, bf16[2,17,16,128]{3,2,1,0:T(8,128)(2,1)S(1)}, u32[]{:S(2)}, u32[]{:S(2)}) collective-permute-start(bf16[2,17,16,128]{3,2,1,0:T(8,128)(2,1)S(1)} %join.1), channel_id=1, source_target_pairs={{0,0},{1,8},{2,16},{3,24},{4,28},{5,20},{6,12},{7,4},{8,1},{9,9},{... | collective-permute-start | bytes 417800 | tf_op jit(solution)/shard_map/ppermute | solution.py:296
  5.8 8.5 %collective-permute-start.3 = (bf16[2,17,16,128]{3,2,1,0:T(8,128)(2,1)S(1)}, bf16[2,17,16,128]{3,2,1,0:T(8,128)(2,1)S(1)}, u32[]{:S(2)}, u32[]{:S(2)}) collective-permute-start(bf16[2,17,16,128]{3,2,1,0:T(8,128)(2,1)S(1)} %join.1), channel_id=1, source_target_pairs={{0,1},{1,0},{2,3},{3,2},{4,6},{5,7},{6,4},{7,5},{8,9},{9,8},{10,11... | collective-permute-start | bytes 417800 | tf_op jit(solution)/shard_map/ppermute | solution.py:296
  10.0 7.8 %collective-permute-start = (bf16[17,16,128]{2,1,0:T(8,128)(2,1)S(1)}, bf16[17,16,128]{2,1,0:T(8,128)(2,1)S(1)}, u32[]{:S(2)}, u32[]{:S(2)}) collective-permute-start(bf16[17,16,128]{2,1,0:T(8,128)(2,1)S(1)} %get-tuple-element.10.own_ref.refs_0_), channel_id=1, source_target_pairs={{0,3},{1,2},{2,1},{3,0},{4,7},{5,6},{6,5},{7,4},{8,11},{9,10},{10,... | collective-permute-start | bytes 208904 | tf_op jit(solution)/shard_map/ppermute | solution.py:296
  13.7 2.1 %collective-permute-start.7 = (bf16[2,17,16,128]{3,2,1,0:T(8,128)(2,1)S(1)}, bf16[2,17,16,128]{3,2,1,0:T(8,128)(2,1)S(1)}, u32[]{:S(2)}, u32[]{:S(2)}) collective-permute-start(bf16[2,17,16,128]{3,2,1,0:T(8,128)(2,1)S(1)} %collective-permute-done.5.refs_2_), channel_id=1, source_target_pairs={{0,4},{1,5},{2,6},{3,7},{4,0},{5,1},{6,2},{7,3},{8,12},{9,13},{10,... | collective-permute-start | bytes 417800 | tf_op jit(solution)/shard_map/ppermute | solution.py:296
  13.8 2.1 %collective-permute-start.8 = (bf16[2,17,16,128]{3,2,1,0:T(8,128)(2,1)S(1)}, bf16[2,17,16,128]{3,2,1,0:T(8,128)(2,1)S(1)}, u32[]{:S(2)}, u32[]{:S(2)}) collective-permute-start(bf16[2,17,16,128]{3,2,1,0:T(8,128)(2,1)S(1)} %collective-permute-done.6.refs_3_), channel_id=1, source_target_pairs={{0,4},{1,5},{2,6},{3,7},{4,0},{5,1},{6,2},{7,3},{8,12},{9,13},{10,... | collective-permute-start | bytes 417800 | tf_op jit(solution)/shard_map/ppermute | solution.py:296
  14.3 3.6 %collective-permute-start.4 = (bf16[17,16,128]{2,1,0:T(8,128)(2,1)S(1)}, bf16[17,16,128]{2,1,0:T(8,128)(2,1)S(1)}, u32[]{:S(2)}, u32[]{:S(2)}) collective-permute-start(bf16[17,16,128]{2,1,0:T(8,128)(2,1)S(1)} %slice_bitcast_fusion), channel_id=1, source_target_pairs={{0,4},{1,5},{2,6},{3,7},{4,0},{5,1},{6,2},{7,3},{8,12},{9,13},{10,... | collective-permute-start | bytes 208904 | tf_op jit(solution)/shard_map/ppermute | solution.py:296

commit v6 on v5

--- a/solution.py
+++ b/solution.py
@@ -113,8 +113,9 @@
 
 
 def exchange_plan(groups):
-    far = [(("far", b), ("far", groups - 1 - b)) for b in reversed(range(groups // 2))]
-    near = [(("near", k), ("near", groups - 1 - k)) for k in range(1, groups // 2)]
+    quarter = groups // 4
+    far = [(("far", b), ("far", b ^ 2 * quarter)) for b in range(quarter, 3 * quarter)]
+    near = [(("near", groups - 1 - k), ("near", k)) for k in range(1, groups // 2)]
     return far + near + [(("near", groups - 1), ("near", groups - 1))]
 
 

time: 19.5 us -> 18.9 us (0.969)
  the two profiles are of different devices: /device:TPU:0 before, /device:TPU:3 now
where the time goes in v6:
time: 18.9 us; the launch traced here: 18.8 us
  starting transfers between devices  11.5 us (61%)
  waiting for transfers between devices  4.04 us (21%)
  Pallas kernels  3.18 us (17%)
    ppermute x9, starting transfers between devices, send(): return lax.ppermute(value, ('chan', 'tm'), route(move))  11.5 us
    ppermute x9, waiting for transfers between devices, send(): return lax.ppermute(value, ('chan', 'tm'), route(move))  4.04 us
    pallas_call x1, Pallas kernels, whiten(): pl.pallas_call(whiten_kernel, out_shape=(pltpu.VMEM((width // LANES + 1,...  1.34 us
    pallas_call x1, Pallas kernels, correlate(): pl.pallas_call(lambda *refs: finish_kernel(groups, *refs), out_shape=jax....  1.31 us
    pallas_call x1, Pallas kernels, correlate(): pl.pallas_call(lambda *refs: gather_kernel(groups, *refs), out_shape=(plt...  0.4 us
  transfers between devices with their start and end apart: 9, of which 3 were waited for; matrix products, arithmetic and copies ran while one was open for 0% of the time, Pallas kernels for 9%

profile of v6, /device:TPU:3, one launch (start us, length us, event | category | flops | bytes accessed | tf_op | source)
XLA Modules:
  0.0 18.8 jit_solution(11996590348572205340)
XLA Ops:
  0.0 0.7 %collective-permute-start.1 = (f32[4,4,2048]{2,1,0:T(4,128)}, f32[4,4,2048]{2,1,0:T(4,128)S(1)}, u32[]{:S(2)}, u32[]{:S(2)}) collective-permute-start(f32[4,4,2048]{2,1,0:T(4,128)} %spectra_ref.1), channel_id=1, source_target_pairs={{0,4},{1,5},{2,6},{3,7},{4,0},{5,1},{6,2},{7,3},{8,12},{9,13},{10,... | collective-permute-start | bytes 393224 | tf_op jit(solution)/shard_map/ppermute | solution.py:297
  0.7 0.0 collective-permute-start.2
  0.7 1.3 %whiten.1 = (bf16[17,16,128]{2,1,0:T(8,128)(2,1)S(1)}, bf16[4,2,256,256]{3,2,1,0:T(8,128)(2,1)S(1)}) custom-call(f32[4,4,2048]{2,1,0:T(4,128)} %spectra_ref.1, s32[4,4]{1,0:T(4,128)} %mask_ref.1, bf16[4,2,256,256]{3,2,1,0:T(8,128)(2,1)} %constant.2.clone.table_ref), custom_call_target="tpu_custom_call" | custom-call | tf_op jit(solution)/shard_map/whiten/pallas_call | solution.py:79
  2.0 0.0 collective-permute-done.2.mask_ref
  2.0 0.0 collective-permute-done.1.spectra_ref
  2.1 0.1 join.1
  2.2 2.3 %collective-permute-start.5 = (bf16[2,17,16,128]{3,2,1,0:T(8,128)(2,1)S(1)}, bf16[2,17,16,128]{3,2,1,0:T(8,128)(2,1)S(1)}, u32[]{:S(2)}, u32[]{:S(2)}) collective-permute-start(bf16[2,17,16,128]{3,2,1,0:T(8,128)(2,1)S(1)} %join.1), channel_id=1, source_target_pairs={{0,8},{1,0},{2,24},{3,16},{4,28},{5,20},{6,12},{7,4},{8,9},{9,1},{... | collective-permute-start | bytes 417800 | tf_op jit(solution)/shard_map/ppermute | solution.py:297
  4.5 4.1 %collective-permute-start.6 = (bf16[2,17,16,128]{3,2,1,0:T(8,128)(2,1)S(1)}, bf16[2,17,16,128]{3,2,1,0:T(8,128)(2,1)S(1)}, u32[]{:S(2)}, u32[]{:S(2)}) collective-permute-start(bf16[2,17,16,128]{3,2,1,0:T(8,128)(2,1)S(1)} %join.1), channel_id=1, source_target_pairs={{0,16},{1,24},{2,0},{3,8},{4,4},{5,12},{6,20},{7,28},{8,17},{9,25}... | collective-permute-start | bytes 417800 | tf_op jit(solution)/shard_map/ppermute | solution.py:297
  8.6 0.1 collective-permute-start.3
  8.7 3.3 %collective-permute-start = (bf16[17,16,128]{2,1,0:T(8,128)(2,1)S(1)}, bf16[17,16,128]{2,1,0:T(8,128)(2,1)S(1)}, u32[]{:S(2)}, u32[]{:S(2)}) collective-permute-start(bf16[17,16,128]{2,1,0:T(8,128)(2,1)S(1)} %get-tuple-element.10.own_ref.refs_0_), channel_id=1, source_target_pairs={{0,3},{1,2},{2,1},{3,0},{4,7},{5,6},{6,5},{7,4},{8,11},{9,10},{10,... | collective-permute-start | bytes 208904 | tf_op jit(solution)/shard_map/ppermute | solution.py:297
  12.0 0.0 collective-permute-done.5.refs_2_
  12.0 0.0 collective-permute-start.7
  12.0 2.2 %collective-permute-done.6.refs_3_ = bf16[2,17,16,128]{3,2,1,0:T(8,128)(2,1)S(1)} collective-permute-done((bf16[2,17,16,128]{3,2,1,0:T(8,128)(2,1)S(1)}, bf16[2,17,16,128]{3,2,1,0:T(8,128)(2,1)S(1)}, u32[]{:S(2)}, u32[]{:S(2)}) %collective-permute-start.6) | collective-permute-done | bytes 139296 | tf_op jit(solution)/shard_map/ppermute | solution.py:297
  14.2 0.0 collective-permute-start.8
  14.2 0.4 %collective-permute-done.3.refs_1_ = bf16[2,17,16,128]{3,2,1,0:T(8,128)(2,1)S(1)} collective-permute-done((bf16[2,17,16,128]{3,2,1,0:T(8,128)(2,1)S(1)}, bf16[2,17,16,128]{3,2,1,0:T(8,128)(2,1)S(1)}, u32[]{:S(2)}, u32[]{:S(2)}) %collective-permute-start.3) | collective-permute-done | bytes 139296 | tf_op jit(solution)/shard_map/ppermute | solution.py:297
  14.6 1.0 %collective-permute-start.4 = (bf16[17,16,128]{2,1,0:T(8,128)(2,1)S(1)}, bf16[17,16,128]{2,1,0:T(8,128)(2,1)S(1)}, u32[]{:S(2)}, u32[]{:S(2)}) collective-permute-start(bf16[17,16,128]{2,1,0:T(8,128)(2,1)S(1)} %slice_bitcast_fusion), channel_id=1, source_target_pairs={{0,4},{1,5},{2,6},{3,7},{4,0},{5,1},{6,2},{7,3},{8,12},{9,13},{10,... | collective-permute-start | bytes 208904 | tf_op jit(solution)/shard_map/ppermute | solution.py:297
  15.6 0.0 collective-permute-done.7.refs_4_
  15.6 0.0 collective-permute-done.8.refs_5_
  15.6 0.4 %gather.1 = (bf16[4,2,17,16,128]{4,3,2,1,0:T(8,128)(2,1)S(1)}, f32[2,8,32,128]{3,2,1,0:T(8,128)S(1)}, f32[32,128]{1,0:T(8,128)S(1)}) custom-call(bf16[17,16,128]{2,1,0:T(8,128)(2,1)S(1)} %get-tuple-element.10.own_ref.refs_0_, bf16[2,17,16,128]{3,2,1,0:T(8,128)(2,1)S(1)} %collective-permute-done.3.refs_1_, ...), custom_call_target="tpu_custom_call" | custom-call | tf_op jit(solution)/shard_map/gather/pallas_call | solution.py:258
  16.0 1.5 %collective-permute-done.refs_0_ = bf16[17,16,128]{2,1,0:T(8,128)(2,1)S(1)} collective-permute-done((bf16[17,16,128]{2,1,0:T(8,128)(2,1)S(1)}, bf16[17,16,128]{2,1,0:T(8,128)(2,1)S(1)}, u32[]{:S(2)}, u32[]{:S(2)}) %collective-permute-start) | collective-permute-done | bytes 69664 | tf_op jit(solution)/shard_map/ppermute | solution.py:297
  17.5 0.0 collective-permute-done.4.refs_1_
  17.5 1.3 %finish.1 = f32[4,8,201]{2,1,0:T(8,128)} custom-call(bf16[17,16,128]{2,1,0:T(8,128)(2,1)S(1)} %collective-permute-done.refs_0_, bf16[17,16,128]{2,1,0:T(8,128)(2,1)S(1)} %collective-permute-done.4.refs_1_, bf16[4,2,17,16,128]{4,3,2,1,0:T(8,128)(2,1)S(1)} %get-tuple-element.11.refs_2_, f32[2,8,32,128]{3,2,1,0:T(8,128)S(1)} %get-tuple-element.12.refs_3_, ...), custom_call_target="tpu_custom_call" | custom-call | tf_op jit(solution)/shard_map/finish/pallas_call | solution.py:271
  (1 shorter events, 0.0 us)
Async XLA Ops:
  0.0 2.0 %collective-permute-start.1 = (f32[4,4,2048]{2,1,0:T(4,128)}, f32[4,4,2048]{2,1,0:T(4,128)S(1)}, u32[]{:S(2)}, u32[]{:S(2)}) collective-permute-start(f32[4,4,2048]{2,1,0:T(4,128)} %spectra_ref.1), channel_id=1, source_target_pairs={{0,4},{1,5},{2,6},{3,7},{4,0},{5,1},{6,2},{7,3},{8,12},{9,13},{10,... | collective-permute-start | bytes 393224 | tf_op jit(solution)/shard_map/ppermute | solution.py:297
  0.7 1.4 %collective-permute-start.2 = (s32[4,4]{1,0:T(4,128)}, s32[4,4]{1,0:T(4,128)S(1)}, u32[]{:S(2)}, u32[]{:S(2)}) collective-permute-start(s32[4,4]{1,0:T(4,128)} %mask_ref.1), channel_id=1, source_target_pairs={{0,4},{1,5},{2,6},{3,7},{4,0},{5,1},{6,2},{7,3},{8,12},{9,13},{10,... | collective-permute-start | bytes 200 | tf_op jit(solution)/shard_map/ppermute | solution.py:297
  2.2 9.9 %collective-permute-start.5 = (bf16[2,17,16,128]{3,2,1,0:T(8,128)(2,1)S(1)}, bf16[2,17,16,128]{3,2,1,0:T(8,128)(2,1)S(1)}, u32[]{:S(2)}, u32[]{:S(2)}) collective-permute-start(bf16[2,17,16,128]{3,2,1,0:T(8,128)(2,1)S(1)} %join.1), channel_id=1, source_target_pairs={{0,8},{1,0},{2,24},{3,16},{4,28},{5,20},{6,12},{7,4},{8,9},{9,1},{... | collective-permute-start | bytes 417800 | tf_op jit(solution)/shard_map/ppermute | solution.py:297
  4.5 9.7 %collective-permute-start.6 = (bf16[2,17,16,128]{3,2,1,0:T(8,128)(2,1)S(1)}, bf16[2,17,16,128]{3,2,1,0:T(8,128)(2,1)S(1)}, u32[]{:S(2)}, u32[]{:S(2)}) collective-permute-start(bf16[2,17,16,128]{3,2,1,0:T(8,128)(2,1)S(1)} %join.1), channel_id=1, source_target_pairs={{0,16},{1,24},{2,0},{3,8},{4,4},{5,12},{6,20},{7,28},{8,17},{9,25}... | collective-permute-start | bytes 417800 | tf_op jit(solution)/shard_map/ppermute | solution.py:297
  8.6 5.9 %collective-permute-start.3 = (bf16[2,17,16,128]{3,2,1,0:T(8,128)(2,1)S(1)}, bf16[2,17,16,128]{3,2,1,0:T(8,128)(2,1)S(1)}, u32[]{:S(2)}, u32[]{:S(2)}) collective-permute-start(bf16[2,17,16,128]{3,2,1,0:T(8,128)(2,1)S(1)} %join.1), channel_id=1, source_target_pairs={{0,2},{1,3},{2,0},{3,1},{4,5},{5,4},{6,7},{7,6},{8,10},{9,11},{10,... | collective-permute-start | bytes 417800 | tf_op jit(solution)/shard_map/ppermute | solution.py:297
  8.7 8.7 %collective-permute-start = (bf16[17,16,128]{2,1,0:T(8,128)(2,1)S(1)}, bf16[17,16,128]{2,1,0:T(8,128)(2,1)S(1)}, u32[]{:S(2)}, u32[]{:S(2)}) collective-permute-start(bf16[17,16,128]{2,1,0:T(8,128)(2,1)S(1)} %get-tuple-element.10.own_ref.refs_0_), channel_id=1, source_target_pairs={{0,3},{1,2},{2,1},{3,0},{4,7},{5,6},{6,5},{7,4},{8,11},{9,10},{10,... | collective-permute-start | bytes 208904 | tf_op jit(solution)/shard_map/ppermute | solution.py:297
  12.0 3.5 %collective-permute-start.7 = (bf16[2,17,16,128]{3,2,1,0:T(8,128)(2,1)S(1)}, bf16[2,17,16,128]{3,2,1,0:T(8,128)(2,1)S(1)}, u32[]{:S(2)}, u32[]{:S(2)}) collective-permute-start(bf16[2,17,16,128]{3,2,1,0:T(8,128)(2,1)S(1)} %collective-permute-done.5.refs_2_), channel_id=1, source_target_pairs={{0,4},{1,5},{2,6},{3,7},{4,0},{5,1},{6,2},{7,3},{8,12},{9,13},{10,... | collective-permute-start | bytes 417800 | tf_op jit(solution)/shard_map/ppermute | solution.py:297
  14.2 1.4 %collective-permute-start.8 = (bf16[2,17,16,128]{3,2,1,0:T(8,128)(2,1)S(1)}, bf16[2,17,16,128]{3,2,1,0:T(8,128)(2,1)S(1)}, u32[]{:S(2)}, u32[]{:S(2)}) collective-permute-start(bf16[2,17,16,128]{3,2,1,0:T(8,128)(2,1)S(1)} %collective-permute-done.6.refs_3_), channel_id=1, source_target_pairs={{0,4},{1,5},{2,6},{3,7},{4,0},{5,1},{6,2},{7,3},{8,12},{9,13},{10,... | collective-permute-start | bytes 417800 | tf_op jit(solution)/shard_map/ppermute | solution.py:297
  14.6 2.9 %collective-permute-start.4 = (bf16[17,16,128]{2,1,0:T(8,128)(2,1)S(1)}, bf16[17,16,128]{2,1,0:T(8,128)(2,1)S(1)}, u32[]{:S(2)}, u32[]{:S(2)}) collective-permute-start(bf16[17,16,128]{2,1,0:T(8,128)(2,1)S(1)} %slice_bitcast_fusion), channel_id=1, source_target_pairs={{0,4},{1,5},{2,6},{3,7},{4,0},{5,1},{6,2},{7,3},{8,12},{9,13},{10,... | collective-permute-start | bytes 208904 | tf_op jit(solution)/shard_map/ppermute | solution.py:297

commit v7 on v6

--- a/solution.py
+++ b/solution.py
@@ -142,11 +142,11 @@
                 pattern_ref[n, fb, 2 * duo + 1] = jnp.where(upper, turned, tile)
 
 
-def tally(slots, far_ref, pattern_ref, cross_ref, pair_ref):
+def tally(slots, far_ref, pattern_ref, cross_ref, span):
     _, blocks, channels, rows, _ = pattern_ref.shape
     half = blocks // 2
     duos = channels // 2
-    for fb in range(half):
+    for fb in span:
         for side in range(2):
             acc = {}
             for n, slot in enumerate(slots):
@@ -168,6 +168,12 @@
                 row = ((i * 2 + side) * duos + duo) * rows
                 for part in range(2):
                     cross_ref[part, fb, row : row + rows] = value[part]
+
+
+def tally_kept(slots, far_ref, pattern_ref, pair_ref):
+    _, blocks, channels, rows, _ = pattern_ref.shape
+    half = blocks // 2
+    duos = channels // 2
     for side in range(2):
         acc = {}
         for n, slot in enumerate(slots):
@@ -205,7 +211,9 @@
             far_ref[mine, side] = direct[side]
             far_ref[theirs, side] = passed[1 - side]
     spread([near_refs[0], *(ref.at[0] for ref in near_refs[1:])], pattern_ref)
-    tally(near_slots(groups, core, True), far_ref, pattern_ref, cross_ref, pair_ref)
+    own = near_slots(groups, core, True)
+    tally(own, far_ref, pattern_ref, cross_ref, range(cross_ref.shape[1]))
+    tally_kept(own, far_ref, pattern_ref, pair_ref)
     for part in range(2):
         for fb in range(cross_ref.shape[1]):
             part_ref[part, fb] = over_windows(cross_ref.at[part, fb], windows)
@@ -219,7 +227,8 @@
     windows = pattern_ref.shape[3] // 2
     core, _ = place(groups)
     spread(late_refs, pattern_ref)
-    tally(near_slots(groups, core, False), far_ref, pattern_ref, cross_ref, pair_ref)
+    brought = near_slots(groups, core, False)
+    tally_kept(brought, far_ref, pattern_ref, pair_ref)
 
     def transform(part, p):
         span = range(p * BLOCK // LANES, (p + 1) * BLOCK // LANES)
@@ -231,7 +240,14 @@
         both = jnp.dot(jnp.concatenate([top, rest], axis=0), held_ref[p, part], preferred_element_type=jnp.float32)
         return both[:size, :LANES] + (both[:size, LANES:] + both[size:, :LANES])
 
-    cosine, sine = [sum(transform(part, p) for p in range(held_ref.shape[0])) for part in range(2)]
+    sums = []
+    for p in range(held_ref.shape[0]):
+        span = range(p * BLOCK // LANES, (p + 1) * BLOCK // LANES)
+        tally(brought, far_ref, pattern_ref, cross_ref, span)
+        if p:
+            sums.append([transform(part, p - 1) for part in range(2)])
+    sums.append([transform(part, p) for part in range(2)])
+    cosine, sine = [sum(parts) for parts in zip(*sums)]
     pairs = jnp.maximum(count_ref[...] + over_windows(pair_ref, windows), 1.0)
     ahead = (cosine - sine) / pairs
     behind = (cosine + sine) / pairs

time: 18.9 us -> 18.9 us (level)
  no operation moved by 1% of the time
where the time goes in v7:
time: 18.9 us; the launch traced here: 18.7 us
  starting transfers between devices  11.5 us (61%)
  waiting for transfers between devices  4.04 us (21%)
  Pallas kernels  3.16 us (17%)
    ppermute x9, starting transfers between devices, send(): return lax.ppermute(value, ('chan', 'tm'), route(move))  11.5 us
    ppermute x9, waiting for transfers between devices, send(): return lax.ppermute(value, ('chan', 'tm'), route(move))  4.04 us
    pallas_call x1, Pallas kernels, whiten(): pl.pallas_call(whiten_kernel, out_shape=(pltpu.VMEM((width // LANES + 1,...  1.34 us
    pallas_call x1, Pallas kernels, correlate(): pl.pallas_call(lambda *refs: finish_kernel(groups, *refs), out_shape=jax....  1.29 us
    pallas_call x1, Pallas kernels, correlate(): pl.pallas_call(lambda *refs: gather_kernel(groups, *refs), out_shape=(plt...  0.4 us
  transfers between devices with their start and end apart: 9, of which 3 were waited for; matrix products, arithmetic and copies ran while one was open for 0% of the time, Pallas kernels for 9%

profile of v7, /device:TPU:3, one launch (start us, length us, event | category | flops | bytes accessed | tf_op | source)
XLA Modules:
  0.0 18.7 jit_solution(630315226255643594)
XLA Ops:
  0.0 0.7 %collective-permute-start.1 = (f32[4,4,2048]{2,1,0:T(4,128)}, f32[4,4,2048]{2,1,0:T(4,128)S(1)}, u32[]{:S(2)}, u32[]{:S(2)}) collective-permute-start(f32[4,4,2048]{2,1,0:T(4,128)} %spectra_ref.1), channel_id=1, source_target_pairs={{0,4},{1,5},{2,6},{3,7},{4,0},{5,1},{6,2},{7,3},{8,12},{9,13},{10,... | collective-permute-start | bytes 393224 | tf_op jit(solution)/shard_map/ppermute | solution.py:313
  0.7 0.0 collective-permute-start.2
  0.7 1.3 %whiten.1 = (bf16[17,16,128]{2,1,0:T(8,128)(2,1)S(1)}, bf16[4,2,256,256]{3,2,1,0:T(8,128)(2,1)S(1)}) custom-call(f32[4,4,2048]{2,1,0:T(4,128)} %spectra_ref.1, s32[4,4]{1,0:T(4,128)} %mask_ref.1, bf16[4,2,256,256]{3,2,1,0:T(8,128)(2,1)} %constant.2.clone.table_ref), custom_call_target="tpu_custom_call" | custom-call | tf_op jit(solution)/shard_map/whiten/pallas_call | solution.py:79
  2.0 0.0 collective-permute-done.2.mask_ref
  2.0 0.0 collective-permute-done.1.spectra_ref
  2.1 0.1 join.1
  2.2 2.3 %collective-permute-start.5 = (bf16[2,17,16,128]{3,2,1,0:T(8,128)(2,1)S(1)}, bf16[2,17,16,128]{3,2,1,0:T(8,128)(2,1)S(1)}, u32[]{:S(2)}, u32[]{:S(2)}) collective-permute-start(bf16[2,17,16,128]{3,2,1,0:T(8,128)(2,1)S(1)} %join.1), channel_id=1, source_target_pairs={{0,8},{1,0},{2,24},{3,16},{4,28},{5,20},{6,12},{7,4},{8,9},{9,1},{... | collective-permute-start | bytes 417800 | tf_op jit(solution)/shard_map/ppermute | solution.py:313
  4.5 4.1 %collective-permute-start.6 = (bf16[2,17,16,128]{3,2,1,0:T(8,128)(2,1)S(1)}, bf16[2,17,16,128]{3,2,1,0:T(8,128)(2,1)S(1)}, u32[]{:S(2)}, u32[]{:S(2)}) collective-permute-start(bf16[2,17,16,128]{3,2,1,0:T(8,128)(2,1)S(1)} %join.1), channel_id=1, source_target_pairs={{0,16},{1,24},{2,0},{3,8},{4,4},{5,12},{6,20},{7,28},{8,17},{9,25}... | collective-permute-start | bytes 417800 | tf_op jit(solution)/shard_map/ppermute | solution.py:313
  8.6 0.1 collective-permute-start.3
  8.7 3.3 %collective-permute-start = (bf16[17,16,128]{2,1,0:T(8,128)(2,1)S(1)}, bf16[17,16,128]{2,1,0:T(8,128)(2,1)S(1)}, u32[]{:S(2)}, u32[]{:S(2)}) collective-permute-start(bf16[17,16,128]{2,1,0:T(8,128)(2,1)S(1)} %get-tuple-element.10.own_ref.refs_0_), channel_id=1, source_target_pairs={{0,3},{1,2},{2,1},{3,0},{4,7},{5,6},{6,5},{7,4},{8,11},{9,10},{10,... | collective-permute-start | bytes 208904 | tf_op jit(solution)/shard_map/ppermute | solution.py:313
  12.0 0.0 collective-permute-done.5.refs_2_
  12.0 0.0 collective-permute-start.7
  12.0 2.2 %collective-permute-done.6.refs_3_ = bf16[2,17,16,128]{3,2,1,0:T(8,128)(2,1)S(1)} collective-permute-done((bf16[2,17,16,128]{3,2,1,0:T(8,128)(2,1)S(1)}, bf16[2,17,16,128]{3,2,1,0:T(8,128)(2,1)S(1)}, u32[]{:S(2)}, u32[]{:S(2)}) %collective-permute-start.6) | collective-permute-done | bytes 139296 | tf_op jit(solution)/shard_map/ppermute | solution.py:313
  14.2 0.0 collective-permute-start.8
  14.2 0.4 %collective-permute-done.3.refs_1_ = bf16[2,17,16,128]{3,2,1,0:T(8,128)(2,1)S(1)} collective-permute-done((bf16[2,17,16,128]{3,2,1,0:T(8,128)(2,1)S(1)}, bf16[2,17,16,128]{3,2,1,0:T(8,128)(2,1)S(1)}, u32[]{:S(2)}, u32[]{:S(2)}) %collective-permute-start.3) | collective-permute-done | bytes 139296 | tf_op jit(solution)/shard_map/ppermute | solution.py:313
  14.6 1.0 %collective-permute-start.4 = (bf16[17,16,128]{2,1,0:T(8,128)(2,1)S(1)}, bf16[17,16,128]{2,1,0:T(8,128)(2,1)S(1)}, u32[]{:S(2)}, u32[]{:S(2)}) collective-permute-start(bf16[17,16,128]{2,1,0:T(8,128)(2,1)S(1)} %slice_bitcast_fusion), channel_id=1, source_target_pairs={{0,4},{1,5},{2,6},{3,7},{4,0},{5,1},{6,2},{7,3},{8,12},{9,13},{10,... | collective-permute-start | bytes 208904 | tf_op jit(solution)/shard_map/ppermute | solution.py:313
  15.6 0.0 collective-permute-done.7.refs_4_
  15.6 0.0 collective-permute-done.8.refs_5_
  15.6 0.4 %gather.1 = (bf16[4,2,17,16,128]{4,3,2,1,0:T(8,128)(2,1)S(1)}, f32[2,8,32,128]{3,2,1,0:T(8,128)S(1)}, f32[32,128]{1,0:T(8,128)S(1)}) custom-call(bf16[17,16,128]{2,1,0:T(8,128)(2,1)S(1)} %get-tuple-element.10.own_ref.refs_0_, bf16[2,17,16,128]{3,2,1,0:T(8,128)(2,1)S(1)} %collective-permute-done.3.refs_1_, ...), custom_call_target="tpu_custom_call" | custom-call | tf_op jit(solution)/shard_map/gather/pallas_call | solution.py:274
  16.0 1.5 %collective-permute-done.refs_0_ = bf16[17,16,128]{2,1,0:T(8,128)(2,1)S(1)} collective-permute-done((bf16[17,16,128]{2,1,0:T(8,128)(2,1)S(1)}, bf16[17,16,128]{2,1,0:T(8,128)(2,1)S(1)}, u32[]{:S(2)}, u32[]{:S(2)}) %collective-permute-start) | collective-permute-done | bytes 69664 | tf_op jit(solution)/shard_map/ppermute | solution.py:313
  17.5 0.0 collective-permute-done.4.refs_1_
  17.5 1.3 %finish.1 = f32[4,8,201]{2,1,0:T(8,128)} custom-call(bf16[17,16,128]{2,1,0:T(8,128)(2,1)S(1)} %collective-permute-done.refs_0_, bf16[17,16,128]{2,1,0:T(8,128)(2,1)S(1)} %collective-permute-done.4.refs_1_, bf16[4,2,17,16,128]{4,3,2,1,0:T(8,128)(2,1)S(1)} %get-tuple-element.11.refs_2_, f32[2,8,32,128]{3,2,1,0:T(8,128)S(1)} %get-tuple-element.12.refs_3_, ...), custom_call_target="tpu_custom_call" | custom-call | tf_op jit(solution)/shard_map/finish/pallas_call | solution.py:287
  (1 shorter events, 0.0 us)
Async XLA Ops:
  0.0 2.0 %collective-permute-start.1 = (f32[4,4,2048]{2,1,0:T(4,128)}, f32[4,4,2048]{2,1,0:T(4,128)S(1)}, u32[]{:S(2)}, u32[]{:S(2)}) collective-permute-start(f32[4,4,2048]{2,1,0:T(4,128)} %spectra_ref.1), channel_id=1, source_target_pairs={{0,4},{1,5},{2,6},{3,7},{4,0},{5,1},{6,2},{7,3},{8,12},{9,13},{10,... | collective-permute-start | bytes 393224 | tf_op jit(solution)/shard_map/ppermute | solution.py:313
  0.7 1.4 %collective-permute-start.2 = (s32[4,4]{1,0:T(4,128)}, s32[4,4]{1,0:T(4,128)S(1)}, u32[]{:S(2)}, u32[]{:S(2)}) collective-permute-start(s32[4,4]{1,0:T(4,128)} %mask_ref.1), channel_id=1, source_target_pairs={{0,4},{1,5},{2,6},{3,7},{4,0},{5,1},{6,2},{7,3},{8,12},{9,13},{10,... | collective-permute-start | bytes 200 | tf_op jit(solution)/shard_map/ppermute | solution.py:313
  2.2 9.9 %collective-permute-start.5 = (bf16[2,17,16,128]{3,2,1,0:T(8,128)(2,1)S(1)}, bf16[2,17,16,128]{3,2,1,0:T(8,128)(2,1)S(1)}, u32[]{:S(2)}, u32[]{:S(2)}) collective-permute-start(bf16[2,17,16,128]{3,2,1,0:T(8,128)(2,1)S(1)} %join.1), channel_id=1, source_target_pairs={{0,8},{1,0},{2,24},{3,16},{4,28},{5,20},{6,12},{7,4},{8,9},{9,1},{... | collective-permute-start | bytes 417800 | tf_op jit(solution)/shard_map/ppermute | solution.py:313
  4.5 9.7 %collective-permute-start.6 = (bf16[2,17,16,128]{3,2,1,0:T(8,128)(2,1)S(1)}, bf16[2,17,16,128]{3,2,1,0:T(8,128)(2,1)S(1)}, u32[]{:S(2)}, u32[]{:S(2)}) collective-permute-start(bf16[2,17,16,128]{3,2,1,0:T(8,128)(2,1)S(1)} %join.1), channel_id=1, source_target_pairs={{0,16},{1,24},{2,0},{3,8},{4,4},{5,12},{6,20},{7,28},{8,17},{9,25}... | collective-permute-start | bytes 417800 | tf_op jit(solution)/shard_map/ppermute | solution.py:313
  8.6 5.9 %collective-permute-start.3 = (bf16[2,17,16,128]{3,2,1,0:T(8,128)(2,1)S(1)}, bf16[2,17,16,128]{3,2,1,0:T(8,128)(2,1)S(1)}, u32[]{:S(2)}, u32[]{:S(2)}) collective-permute-start(bf16[2,17,16,128]{3,2,1,0:T(8,128)(2,1)S(1)} %join.1), channel_id=1, source_target_pairs={{0,2},{1,3},{2,0},{3,1},{4,5},{5,4},{6,7},{7,6},{8,10},{9,11},{10,... | collective-permute-start | bytes 417800 | tf_op jit(solution)/shard_map/ppermute | solution.py:313
  8.7 8.7 %collective-permute-start = (bf16[17,16,128]{2,1,0:T(8,128)(2,1)S(1)}, bf16[17,16,128]{2,1,0:T(8,128)(2,1)S(1)}, u32[]{:S(2)}, u32[]{:S(2)}) collective-permute-start(bf16[17,16,128]{2,1,0:T(8,128)(2,1)S(1)} %get-tuple-element.10.own_ref.refs_0_), channel_id=1, source_target_pairs={{0,3},{1,2},{2,1},{3,0},{4,7},{5,6},{6,5},{7,4},{8,11},{9,10},{10,... | collective-permute-start | bytes 208904 | tf_op jit(solution)/shard_map/ppermute | solution.py:313
  12.0 3.5 %collective-permute-start.7 = (bf16[2,17,16,128]{3,2,1,0:T(8,128)(2,1)S(1)}, bf16[2,17,16,128]{3,2,1,0:T(8,128)(2,1)S(1)}, u32[]{:S(2)}, u32[]{:S(2)}) collective-permute-start(bf16[2,17,16,128]{3,2,1,0:T(8,128)(2,1)S(1)} %collective-permute-done.5.refs_2_), channel_id=1, source_target_pairs={{0,4},{1,5},{2,6},{3,7},{4,0},{5,1},{6,2},{7,3},{8,12},{9,13},{10,... | collective-permute-start | bytes 417800 | tf_op jit(solution)/shard_map/ppermute | solution.py:313
  14.2 1.4 %collective-permute-start.8 = (bf16[2,17,16,128]{3,2,1,0:T(8,128)(2,1)S(1)}, bf16[2,17,16,128]{3,2,1,0:T(8,128)(2,1)S(1)}, u32[]{:S(2)}, u32[]{:S(2)}) collective-permute-start(bf16[2,17,16,128]{3,2,1,0:T(8,128)(2,1)S(1)} %collective-permute-done.6.refs_3_), channel_id=1, source_target_pairs={{0,4},{1,5},{2,6},{3,7},{4,0},{5,1},{6,2},{7,3},{8,12},{9,13},{10,... | collective-permute-start | bytes 417800 | tf_op jit(solution)/shard_map/ppermute | solution.py:313
  14.6 2.9 %collective-permute-start.4 = (bf16[17,16,128]{2,1,0:T(8,128)(2,1)S(1)}, bf16[17,16,128]{2,1,0:T(8,128)(2,1)S(1)}, u32[]{:S(2)}, u32[]{:S(2)}) collective-permute-start(bf16[17,16,128]{2,1,0:T(8,128)(2,1)S(1)} %slice_bitcast_fusion), channel_id=1, source_target_pairs={{0,4},{1,5},{2,6},{3,7},{4,0},{5,1},{6,2},{7,3},{8,12},{9,13},{10,... | collective-permute-start | bytes 208904 | tf_op jit(solution)/shard_map/ppermute | solution.py:313

commit v8 on v6

--- a/solution.py
+++ b/solution.py
@@ -311,7 +311,8 @@
 
             return send(value, move)
 
-        sibling = swap(spectra), swap(keep_mask)
+        kept = swap(keep_mask)
+        sibling = swap(spectra), kept
         own, table = whiten(spectra, keep_mask, jnp.asarray(lag_table(width // 2)))
         chip = join(own, *sibling)
         plan = exchange_plan(groups)

time: 18.9 us -> 18.9 us (level)
  no operation moved by 1% of the time
where the time goes in v8:
time: 18.9 us; the launch traced here: 18.8 us
  starting transfers between devices  11.5 us (61%)
  waiting for transfers between devices  4.04 us (21%)
  Pallas kernels  3.18 us (17%)
    ppermute x9, starting transfers between devices, send(): return lax.ppermute(value, ('chan', 'tm'), route(move))  11.5 us
    ppermute x9, waiting for transfers between devices, send(): return lax.ppermute(value, ('chan', 'tm'), route(move))  4.04 us
    pallas_call x1, Pallas kernels, whiten(): pl.pallas_call(whiten_kernel, out_shape=(pltpu.VMEM((width // LANES + 1,...  1.34 us
    pallas_call x1, Pallas kernels, correlate(): pl.pallas_call(lambda *refs: finish_kernel(groups, *refs), out_shape=jax....  1.31 us
    pallas_call x1, Pallas kernels, correlate(): pl.pallas_call(lambda *refs: gather_kernel(groups, *refs), out_shape=(plt...  0.4 us
  transfers between devices with their start and end apart: 9, of which 3 were waited for; matrix products, arithmetic and copies ran while one was open for 0% of the time, Pallas kernels for 9%

profile of v8, /device:TPU:3, one launch (start us, length us, event | category | flops | bytes accessed | tf_op | source)
XLA Modules:
  0.0 18.8 jit_solution(11996590348572205340)
XLA Ops:
  0.0 0.7 %collective-permute-start.1 = (f32[4,4,2048]{2,1,0:T(4,128)}, f32[4,4,2048]{2,1,0:T(4,128)S(1)}, u32[]{:S(2)}, u32[]{:S(2)}) collective-permute-start(f32[4,4,2048]{2,1,0:T(4,128)} %spectra_ref.1), channel_id=1, source_target_pairs={{0,4},{1,5},{2,6},{3,7},{4,0},{5,1},{6,2},{7,3},{8,12},{9,13},{10,... | collective-permute-start | bytes 393224 | tf_op jit(solution)/shard_map/ppermute | solution.py:297
  0.7 0.0 collective-permute-start.2
  0.7 1.3 %whiten.1 = (bf16[17,16,128]{2,1,0:T(8,128)(2,1)S(1)}, bf16[4,2,256,256]{3,2,1,0:T(8,128)(2,1)S(1)}) custom-call(f32[4,4,2048]{2,1,0:T(4,128)} %spectra_ref.1, s32[4,4]{1,0:T(4,128)} %mask_ref.1, bf16[4,2,256,256]{3,2,1,0:T(8,128)(2,1)} %constant.2.clone.table_ref), custom_call_target="tpu_custom_call" | custom-call | tf_op jit(solution)/shard_map/whiten/pallas_call | solution.py:79
  2.0 0.0 collective-permute-done.2.mask_ref
  2.0 0.0 collective-permute-done.1.spectra_ref
  2.1 0.1 join.1
  2.2 2.3 %collective-permute-start.5 = (bf16[2,17,16,128]{3,2,1,0:T(8,128)(2,1)S(1)}, bf16[2,17,16,128]{3,2,1,0:T(8,128)(2,1)S(1)}, u32[]{:S(2)}, u32[]{:S(2)}) collective-permute-start(bf16[2,17,16,128]{3,2,1,0:T(8,128)(2,1)S(1)} %join.1), channel_id=1, source_target_pairs={{0,8},{1,0},{2,24},{3,16},{4,28},{5,20},{6,12},{7,4},{8,9},{9,1},{... | collective-permute-start | bytes 417800 | tf_op jit(solution)/shard_map/ppermute | solution.py:297
  4.5 4.1 %collective-permute-start.6 = (bf16[2,17,16,128]{3,2,1,0:T(8,128)(2,1)S(1)}, bf16[2,17,16,128]{3,2,1,0:T(8,128)(2,1)S(1)}, u32[]{:S(2)}, u32[]{:S(2)}) collective-permute-start(bf16[2,17,16,128]{3,2,1,0:T(8,128)(2,1)S(1)} %join.1), channel_id=1, source_target_pairs={{0,16},{1,24},{2,0},{3,8},{4,4},{5,12},{6,20},{7,28},{8,17},{9,25}... | collective-permute-start | bytes 417800 | tf_op jit(solution)/shard_map/ppermute | solution.py:297
  8.6 0.1 collective-permute-start.3
  8.7 3.3 %collective-permute-start = (bf16[17,16,128]{2,1,0:T(8,128)(2,1)S(1)}, bf16[17,16,128]{2,1,0:T(8,128)(2,1)S(1)}, u32[]{:S(2)}, u32[]{:S(2)}) collective-permute-start(bf16[17,16,128]{2,1,0:T(8,128)(2,1)S(1)} %get-tuple-element.10.own_ref.refs_0_), channel_id=1, source_target_pairs={{0,3},{1,2},{2,1},{3,0},{4,7},{5,6},{6,5},{7,4},{8,11},{9,10},{10,... | collective-permute-start | bytes 208904 | tf_op jit(solution)/shard_map/ppermute | solution.py:297
  12.0 0.0 collective-permute-done.5.refs_2_
  12.0 0.0 collective-permute-start.7
  12.0 2.2 %collective-permute-done.6.refs_3_ = bf16[2,17,16,128]{3,2,1,0:T(8,128)(2,1)S(1)} collective-permute-done((bf16[2,17,16,128]{3,2,1,0:T(8,128)(2,1)S(1)}, bf16[2,17,16,128]{3,2,1,0:T(8,128)(2,1)S(1)}, u32[]{:S(2)}, u32[]{:S(2)}) %collective-permute-start.6) | collective-permute-done | bytes 139296 | tf_op jit(solution)/shard_map/ppermute | solution.py:297
  14.2 0.0 collective-permute-start.8
  14.2 0.4 %collective-permute-done.3.refs_1_ = bf16[2,17,16,128]{3,2,1,0:T(8,128)(2,1)S(1)} collective-permute-done((bf16[2,17,16,128]{3,2,1,0:T(8,128)(2,1)S(1)}, bf16[2,17,16,128]{3,2,1,0:T(8,128)(2,1)S(1)}, u32[]{:S(2)}, u32[]{:S(2)}) %collective-permute-start.3) | collective-permute-done | bytes 139296 | tf_op jit(solution)/shard_map/ppermute | solution.py:297
  14.6 1.0 %collective-permute-start.4 = (bf16[17,16,128]{2,1,0:T(8,128)(2,1)S(1)}, bf16[17,16,128]{2,1,0:T(8,128)(2,1)S(1)}, u32[]{:S(2)}, u32[]{:S(2)}) collective-permute-start(bf16[17,16,128]{2,1,0:T(8,128)(2,1)S(1)} %slice_bitcast_fusion), channel_id=1, source_target_pairs={{0,4},{1,5},{2,6},{3,7},{4,0},{5,1},{6,2},{7,3},{8,12},{9,13},{10,... | collective-permute-start | bytes 208904 | tf_op jit(solution)/shard_map/ppermute | solution.py:297
  15.6 0.0 collective-permute-done.7.refs_4_
  15.6 0.0 collective-permute-done.8.refs_5_
  15.6 0.4 %gather.1 = (bf16[4,2,17,16,128]{4,3,2,1,0:T(8,128)(2,1)S(1)}, f32[2,8,32,128]{3,2,1,0:T(8,128)S(1)}, f32[32,128]{1,0:T(8,128)S(1)}) custom-call(bf16[17,16,128]{2,1,0:T(8,128)(2,1)S(1)} %get-tuple-element.10.own_ref.refs_0_, bf16[2,17,16,128]{3,2,1,0:T(8,128)(2,1)S(1)} %collective-permute-done.3.refs_1_, ...), custom_call_target="tpu_custom_call" | custom-call | tf_op jit(solution)/shard_map/gather/pallas_call | solution.py:258
  16.0 1.5 %collective-permute-done.refs_0_ = bf16[17,16,128]{2,1,0:T(8,128)(2,1)S(1)} collective-permute-done((bf16[17,16,128]{2,1,0:T(8,128)(2,1)S(1)}, bf16[17,16,128]{2,1,0:T(8,128)(2,1)S(1)}, u32[]{:S(2)}, u32[]{:S(2)}) %collective-permute-start) | collective-permute-done | bytes 69664 | tf_op jit(solution)/shard_map/ppermute | solution.py:297
  17.5 0.0 collective-permute-done.4.refs_1_
  17.5 1.3 %finish.1 = f32[4,8,201]{2,1,0:T(8,128)} custom-call(bf16[17,16,128]{2,1,0:T(8,128)(2,1)S(1)} %collective-permute-done.refs_0_, bf16[17,16,128]{2,1,0:T(8,128)(2,1)S(1)} %collective-permute-done.4.refs_1_, bf16[4,2,17,16,128]{4,3,2,1,0:T(8,128)(2,1)S(1)} %get-tuple-element.11.refs_2_, f32[2,8,32,128]{3,2,1,0:T(8,128)S(1)} %get-tuple-element.12.refs_3_, ...), custom_call_target="tpu_custom_call" | custom-call | tf_op jit(solution)/shard_map/finish/pallas_call | solution.py:271
  (1 shorter events, 0.0 us)
Async XLA Ops:
  0.0 2.0 %collective-permute-start.1 = (f32[4,4,2048]{2,1,0:T(4,128)}, f32[4,4,2048]{2,1,0:T(4,128)S(1)}, u32[]{:S(2)}, u32[]{:S(2)}) collective-permute-start(f32[4,4,2048]{2,1,0:T(4,128)} %spectra_ref.1), channel_id=1, source_target_pairs={{0,4},{1,5},{2,6},{3,7},{4,0},{5,1},{6,2},{7,3},{8,12},{9,13},{10,... | collective-permute-start | bytes 393224 | tf_op jit(solution)/shard_map/ppermute | solution.py:297
  0.7 1.4 %collective-permute-start.2 = (s32[4,4]{1,0:T(4,128)}, s32[4,4]{1,0:T(4,128)S(1)}, u32[]{:S(2)}, u32[]{:S(2)}) collective-permute-start(s32[4,4]{1,0:T(4,128)} %mask_ref.1), channel_id=1, source_target_pairs={{0,4},{1,5},{2,6},{3,7},{4,0},{5,1},{6,2},{7,3},{8,12},{9,13},{10,... | collective-permute-start | bytes 200 | tf_op jit(solution)/shard_map/ppermute | solution.py:297
  2.2 9.9 %collective-permute-start.5 = (bf16[2,17,16,128]{3,2,1,0:T(8,128)(2,1)S(1)}, bf16[2,17,16,128]{3,2,1,0:T(8,128)(2,1)S(1)}, u32[]{:S(2)}, u32[]{:S(2)}) collective-permute-start(bf16[2,17,16,128]{3,2,1,0:T(8,128)(2,1)S(1)} %join.1), channel_id=1, source_target_pairs={{0,8},{1,0},{2,24},{3,16},{4,28},{5,20},{6,12},{7,4},{8,9},{9,1},{... | collective-permute-start | bytes 417800 | tf_op jit(solution)/shard_map/ppermute | solution.py:297
  4.5 9.7 %collective-permute-start.6 = (bf16[2,17,16,128]{3,2,1,0:T(8,128)(2,1)S(1)}, bf16[2,17,16,128]{3,2,1,0:T(8,128)(2,1)S(1)}, u32[]{:S(2)}, u32[]{:S(2)}) collective-permute-start(bf16[2,17,16,128]{3,2,1,0:T(8,128)(2,1)S(1)} %join.1), channel_id=1, source_target_pairs={{0,16},{1,24},{2,0},{3,8},{4,4},{5,12},{6,20},{7,28},{8,17},{9,25}... | collective-permute-start | bytes 417800 | tf_op jit(solution)/shard_map/ppermute | solution.py:297
  8.6 5.9 %collective-permute-start.3 = (bf16[2,17,16,128]{3,2,1,0:T(8,128)(2,1)S(1)}, bf16[2,17,16,128]{3,2,1,0:T(8,128)(2,1)S(1)}, u32[]{:S(2)}, u32[]{:S(2)}) collective-permute-start(bf16[2,17,16,128]{3,2,1,0:T(8,128)(2,1)S(1)} %join.1), channel_id=1, source_target_pairs={{0,2},{1,3},{2,0},{3,1},{4,5},{5,4},{6,7},{7,6},{8,10},{9,11},{10,... | collective-permute-start | bytes 417800 | tf_op jit(solution)/shard_map/ppermute | solution.py:297
  8.7 8.7 %collective-permute-start = (bf16[17,16,128]{2,1,0:T(8,128)(2,1)S(1)}, bf16[17,16,128]{2,1,0:T(8,128)(2,1)S(1)}, u32[]{:S(2)}, u32[]{:S(2)}) collective-permute-start(bf16[17,16,128]{2,1,0:T(8,128)(2,1)S(1)} %get-tuple-element.10.own_ref.refs_0_), channel_id=1, source_target_pairs={{0,3},{1,2},{2,1},{3,0},{4,7},{5,6},{6,5},{7,4},{8,11},{9,10},{10,... | collective-permute-start | bytes 208904 | tf_op jit(solution)/shard_map/ppermute | solution.py:297
  12.0 3.5 %collective-permute-start.7 = (bf16[2,17,16,128]{3,2,1,0:T(8,128)(2,1)S(1)}, bf16[2,17,16,128]{3,2,1,0:T(8,128)(2,1)S(1)}, u32[]{:S(2)}, u32[]{:S(2)}) collective-permute-start(bf16[2,17,16,128]{3,2,1,0:T(8,128)(2,1)S(1)} %collective-permute-done.5.refs_2_), channel_id=1, source_target_pairs={{0,4},{1,5},{2,6},{3,7},{4,0},{5,1},{6,2},{7,3},{8,12},{9,13},{10,... | collective-permute-start | bytes 417800 | tf_op jit(solution)/shard_map/ppermute | solution.py:297
  14.2 1.4 %collective-permute-start.8 = (bf16[2,17,16,128]{3,2,1,0:T(8,128)(2,1)S(1)}, bf16[2,17,16,128]{3,2,1,0:T(8,128)(2,1)S(1)}, u32[]{:S(2)}, u32[]{:S(2)}) collective-permute-start(bf16[2,17,16,128]{3,2,1,0:T(8,128)(2,1)S(1)} %collective-permute-done.6.refs_3_), channel_id=1, source_target_pairs={{0,4},{1,5},{2,6},{3,7},{4,0},{5,1},{6,2},{7,3},{8,12},{9,13},{10,... | collective-permute-start | bytes 417800 | tf_op jit(solution)/shard_map/ppermute | solution.py:297
  14.6 2.9 %collective-permute-start.4 = (bf16[17,16,128]{2,1,0:T(8,128)(2,1)S(1)}, bf16[17,16,128]{2,1,0:T(8,128)(2,1)S(1)}, u32[]{:S(2)}, u32[]{:S(2)}) collective-permute-start(bf16[17,16,128]{2,1,0:T(8,128)(2,1)S(1)} %slice_bitcast_fusion), channel_id=1, source_target_pairs={{0,4},{1,5},{2,6},{3,7},{4,0},{5,1},{6,2},{7,3},{8,12},{9,13},{10,... | collective-permute-start | bytes 208904 | tf_op jit(solution)/shard_map/ppermute | solution.py:297
